TPU v7x, 32 devices: a whole 2x2x4 slice. The times are simulated.
32 devices in a mesh: spec: 4 (over y, core), wave: 8 (over z, x).
Axes of the slice: x: 2, y: 2, z: 4, core: 2. Of those that a mesh axis runs over, the one named last changes fastest.
Arguments:
- templates: float32 [48, 10, 4096], P('spec', None, 'wave'), as said below
- resolution: float32 [256, 11, 4096], P('spec', None, 'wave'), may hold values from 0.02 to 0.2
- coadd_flux: float32 [256, 4096], P('spec', 'wave'), as said below
- coadd_ivar: float32 [256, 4096], P('spec', 'wave'), may hold values from 0.1 to 2
- best_index: int32 [256], P('spec'), may hold values from 0 to 47, as said below
- exposures: float32 [256, 3, 4096], P(('spec', 'wave')), may hold values from -6 to 6
- exposure_mask: int32 [256, 3, 4096], P(('spec', 'wave')), may hold values 0 or 1
Outputs:
- fit_gain: float32 [256, 48], P(('spec', 'wave'))
- residuals: float32 [256, 3, 4096], P(('spec', 'wave'))
Inputs may be any that keep to these rules, and one draw needn't show every extreme that they name: Redshifted templates, one set of 10 for each of the 48 redshifts. `coadd_flux`: coadded flux of each spectrum. `best_index`: an index into the 48 redshifts.
All inputs are finite; a program needn't handle non-finite values. No bound on the sum of `exposure_mask` on one device may be relied on, other than what follows from the above.
Results may differ from a plain program's by a relative error of at most 0.000073.
Values sent between devices are 32-bit elements; how exact they have to be, the bound alone decides.
No kernel may reach another device: no remote copies, remote signals or barrier semaphores. Data moves between devices by JAX's collectives and lax.ppermute only.
A program may use at most 192 MiB of HBM per device.

v0:
```python
import math

import jax
import jax.numpy as jnp
from jax import lax
from jax.sharding import PartitionSpec as P


def padded_2(shard, sides, width):
    for axis, dim in sides:
        count, length = (lax.axis_size(axis), shard.shape[dim])
        up = [(i, (i + 1) % count) for i in range(count - 1)]
        down = [(j, i) for i, j in up]
        last = lax.slice_in_dim(shard, length - width, length, axis=dim)
        first = lax.slice_in_dim(shard, 0, width, axis=dim)
        before = lax.ppermute(last, axis, up)
        after = lax.ppermute(first, axis, down)
        shard = jnp.concatenate([before, shard, after], axis=dim)
    return shard


def body(templates, resolution, coadd_flux, coadd_ivar, best_index, exposures, exposure_mask):
    spectra_dev, band_count, pixel_width = resolution.shape
    half_band = band_count // 2
    templ_count = templates.shape[1]
    redshifts = templates.shape[0] * lax.axis_size("spec")
    own_rows = spectra_dev // lax.axis_size("wave")
    full_count = templ_count * templ_count
    columns = full_count + templ_count
    weight_root = jnp.sqrt(coadd_ivar)
    weighted_band = resolution * weight_root[:, None, :]
    target = coadd_flux * weight_root
    padded = padded_2(templates, (("wave", 2),), half_band)

    def block_terms(source):
        weighted_basis = weighted_band[:, 0, None, None, :] * source[None, :, :, 0:pixel_width]
        for offset in range(1, band_count):
            weighted_basis = (
                weighted_basis
                + weighted_band[:, offset, None, None, :]
                * source[None, :, :, offset : offset + pixel_width]
            )
        normal = jnp.einsum(
            "szkp,szlp->szkl", weighted_basis, weighted_basis, precision=lax.Precision.HIGHEST
        )
        projection = jnp.einsum(
            "szkp,sp->szk", weighted_basis, target, precision=lax.Precision.HIGHEST
        )
        flattened = normal.reshape(normal.shape[0], normal.shape[1], full_count)
        return jnp.concatenate([flattened, projection], axis=2)

    shard_piece = lax.all_gather(padded, "spec", axis=0, tiled=True)
    piece_rows = shard_piece.shape[0]
    step_rows = math.gcd(piece_rows, 16)
    grouped = shard_piece.reshape(
        piece_rows // step_rows, step_rows, templ_count, shard_piece.shape[2]
    )
    results = lax.map(block_terms, grouped)
    values = jnp.transpose(results, (1, 0, 2, 3)).reshape(spectra_dev, piece_rows * columns)
    partials = values
    positions = jnp.arange(piece_rows, dtype=jnp.int32)
    selector = (best_index[:, None] == positions[None, :]).astype(jnp.float32)
    picked = jnp.einsum("sz,zkp->skp", selector, shard_piece, precision=lax.Precision.HIGHEST)
    partials, picked = (partials, picked)
    summed = lax.psum_scatter(partials, "wave", scatter_dimension=0, tiled=True).reshape(
        own_rows, redshifts, columns
    )
    normal = summed[:, :, :full_count]
    normal = normal.reshape(own_rows, redshifts, templ_count, templ_count)
    projection = summed[:, :, full_count:]
    factor = jnp.linalg.cholesky(normal)
    coefficients = jax.scipy.linalg.cho_solve((factor, True), projection[..., None])[..., 0]
    fit_gain = jnp.log1p(jnp.sum(projection * coefficients, axis=2) / templ_count)
    own_start = lax.axis_index("wave") * own_rows
    own_best = lax.dynamic_slice_in_dim(best_index, own_start, own_rows)
    chooser = (own_best[:, None] == jnp.arange(redshifts, dtype=jnp.int32)[None, :]).astype(
        jnp.float32
    )
    best_coef = jnp.einsum("sz,szk->sk", chooser, coefficients, precision=lax.Precision.HIGHEST)
    best_basis = resolution[:, 0, None, :] * picked[:, :, 0:pixel_width]
    for offset in range(1, band_count):
        best_basis = (
            best_basis
            + resolution[:, offset, None, :] * picked[:, :, offset : offset + pixel_width]
        )
    relayed = lax.all_to_all(best_basis, "wave", split_axis=0, concat_axis=2, tiled=True)
    model_rows = jnp.einsum("sk,skp->sp", best_coef, relayed, precision=lax.Precision.HIGHEST)
    residuals = exposure_mask.astype(jnp.float32) * (exposures - model_rows[:, None, :])
    return (fit_gain, residuals)


def solution(mesh):
    in_specs = (
        P("spec", None, "wave"),
        P("spec", None, "wave"),
        P("spec", "wave"),
        P("spec", "wave"),
        P("spec"),
        P(("spec", "wave"), None, None),
        P(("spec", "wave"), None, None),
    )
    out_specs = (P(("spec", "wave"), None), P(("spec", "wave"), None, None))
    return jax.shard_map(body, mesh=mesh, in_specs=in_specs, out_specs=out_specs, check_vma=False)
```

profile of v0, /device:TPU:0, one launch (start us, length us, event | category | flops | bytes accessed | tf_op | source)
XLA Modules:
  0.0 1279.3 jit_solution(5725878150896086762)
XLA Ops:
  9.7 5.5 collective-permute-start
  22.3 16.0 %all_gather.3 = f32[48,10,522]{2,1,0:T(8,128)} all-gather(f32[12,10,522]{2,1,0:T(8,128)S(1)} %pad_maximum_fusion), channel_id=1, replica_groups=mesh['spec'=4,'wave'=8] {'spec'}, dimensions={0}, use_global_device_ids=true | all-gather | bytes 1252800 | tf_op jit(solution)/shard_map/all_gather | solution.py:52
  38.3 753.3 %while.10 = (s32[]{:T(128)}, f32[3,64,16,110]{1,2,3,0:T(8,128)}, f32[64,11,512]{2,0,1:T(8,128)}, f32[3,16,10,522]{3,2,1,0:T(8,128)}, f32[64,512]{1,0:T(8,128)}, /*index=5*/s32[]{:T(128)}) while((s32[]{:T(128)}, f32[3,64,16,110]{1,2,3,0:T(8,128)}, f32[64,11,512]{2,0,1:T(8,128)}, f32[3,16,10,522]{3,2,1,0:T(8,128)}, f32[64,512]{1,0:T(8,128)}, ...), condition=%wide.region_1.2_spmd, body=%wide.region_0.1_spmd.sunk | while | flops 912373760 | bytes 82834456 | solution.py:58
  43.1 153.8 %fusion.42 = f32[64,1,16,10]{3,1,2,0:T(1,128)} fusion(f32[16,10,512]{2,1,0:T(8,128)S(1)} %get-tuple-element.140, f32[64,512]{1,0:T(8,128)S(1)} %get-tuple-element.141, f32[16,10,512]{2,1,0:T(8,128)S(1)} %get-tuple-element.142, f32[64,512]{1,0:T(8,128)S(1)} %get-tuple-element.143, f32[16,10,512]{2,1,0:T(8,128)S(1)} %get-tuple-element.144, ...), kind=kOutput, calls=%fused_computation.1.clone.1 | convolution fusion | flops 173015040 | bytes 5218304 | tf_op jit(solution)/shard_map/while/body/eval_jaxpr/szkp,sp->szk/dot_general | solution.py:46
  198.8 27.6 %multiply_add_fusion.11 = f32[64,16,10,512]{3,2,1,0:T(8,128)} fusion(f32[16,10,512]{2,1,0:T(8,128)S(1)} %get-tuple-element.140, f32[64,512]{1,0:T(8,128)S(1)} %get-tuple-element.141, f32[16,10,512]{2,1,0:T(8,128)S(1)} %get-tuple-element.142, f32[64,512]{1,0:T(8,128)S(1)} %get-tuple-element.143, ...), kind=kLoop, calls=%fused_computation.clone.1.clone.2.clone.1 | loop fusion | flops 110100480 | bytes 26017792 | tf_op jit(solution)/shard_map/while/body/eval_jaxpr/szkp,szlp->szkl/dot_general | solution.py:43
  226.5 40.4 %fusion.43 = f32[64,16,10,10]{3,2,1,0:T(8,128)} fusion(f32[64,16,10,512]{3,2,1,0:T(8,128)} %multiply_add_fusion.11), kind=kOutput, calls=%fused_computation.2.clone.3 | convolution fusion | flops 629145600 | bytes 21381120 | tf_op jit(solution)/shard_map/while/body/eval_jaxpr/szkp,szlp->szkl/dot_general | solution.py:43
  266.9 6.9 copy.80
  298.2 153.8 %fusion.42 = f32[64,1,16,10]{3,1,2,0:T(1,128)} fusion(f32[16,10,512]{2,1,0:T(8,128)S(1)} %get-tuple-element.140, f32[64,512]{1,0:T(8,128)S(1)} %get-tuple-element.141, f32[16,10,512]{2,1,0:T(8,128)S(1)} %get-tuple-element.142, f32[64,512]{1,0:T(8,128)S(1)} %get-tuple-element.143, f32[16,10,512]{2,1,0:T(8,128)S(1)} %get-tuple-element.144, ...), kind=kOutput, calls=%fused_computation.1.clone.1 | convolution fusion | flops 173015040 | bytes 5218304 | tf_op jit(solution)/shard_map/while/body/eval_jaxpr/szkp,sp->szk/dot_general | solution.py:46
  454.0 27.6 %multiply_add_fusion.11 = f32[64,16,10,512]{3,2,1,0:T(8,128)} fusion(f32[16,10,512]{2,1,0:T(8,128)S(1)} %get-tuple-element.140, f32[64,512]{1,0:T(8,128)S(1)} %get-tuple-element.141, f32[16,10,512]{2,1,0:T(8,128)S(1)} %get-tuple-element.142, f32[64,512]{1,0:T(8,128)S(1)} %get-tuple-element.143, ...), kind=kLoop, calls=%fused_computation.clone.1.clone.2.clone.1 | loop fusion | flops 110100480 | bytes 26017792 | tf_op jit(solution)/shard_map/while/body/eval_jaxpr/szkp,szlp->szkl/dot_general | solution.py:43
  481.6 40.4 %fusion.43 = f32[64,16,10,10]{3,2,1,0:T(8,128)} fusion(f32[64,16,10,512]{3,2,1,0:T(8,128)} %multiply_add_fusion.11), kind=kOutput, calls=%fused_computation.2.clone.3 | convolution fusion | flops 629145600 | bytes 21381120 | tf_op jit(solution)/shard_map/while/body/eval_jaxpr/szkp,szlp->szkl/dot_general | solution.py:43
  522.0 6.9 copy.80
  553.4 153.8 %fusion.42 = f32[64,1,16,10]{3,1,2,0:T(1,128)} fusion(f32[16,10,512]{2,1,0:T(8,128)S(1)} %get-tuple-element.140, f32[64,512]{1,0:T(8,128)S(1)} %get-tuple-element.141, f32[16,10,512]{2,1,0:T(8,128)S(1)} %get-tuple-element.142, f32[64,512]{1,0:T(8,128)S(1)} %get-tuple-element.143, f32[16,10,512]{2,1,0:T(8,128)S(1)} %get-tuple-element.144, ...), kind=kOutput, calls=%fused_computation.1.clone.1 | convolution fusion | flops 173015040 | bytes 5218304 | tf_op jit(solution)/shard_map/while/body/eval_jaxpr/szkp,sp->szk/dot_general | solution.py:46
  709.2 27.6 %multiply_add_fusion.11 = f32[64,16,10,512]{3,2,1,0:T(8,128)} fusion(f32[16,10,512]{2,1,0:T(8,128)S(1)} %get-tuple-element.140, f32[64,512]{1,0:T(8,128)S(1)} %get-tuple-element.141, f32[16,10,512]{2,1,0:T(8,128)S(1)} %get-tuple-element.142, f32[64,512]{1,0:T(8,128)S(1)} %get-tuple-element.143, ...), kind=kLoop, calls=%fused_computation.clone.1.clone.2.clone.1 | loop fusion | flops 110100480 | bytes 26017792 | tf_op jit(solution)/shard_map/while/body/eval_jaxpr/szkp,szlp->szkl/dot_general | solution.py:43
  736.8 40.4 %fusion.43 = f32[64,16,10,10]{3,2,1,0:T(8,128)} fusion(f32[64,16,10,512]{3,2,1,0:T(8,128)} %multiply_add_fusion.11), kind=kOutput, calls=%fused_computation.2.clone.3 | convolution fusion | flops 629145600 | bytes 21381120 | tf_op jit(solution)/shard_map/while/body/eval_jaxpr/szkp,szlp->szkl/dot_general | solution.py:43
  777.2 6.9 copy.80
  795.9 2.8 fusion.16
  798.8 3.6 fusion.6
  804.6 5.7 all-to-all-start
  810.4 55.5 %all-to-all-done = f32[64,10,512]{2,1,0:T(8,128)S(1)} async-done(((f32[64,10,512]{2,1,0:T(8,128)}), f32[64,10,512]{2,1,0:T(8,128)S(1)}, u32[]{:S(2)}, u32[]{:S(2)}) %all-to-all-start) | async-done | bytes 1310752 | tf_op jit(solution)/shard_map/all_to_all | solution.py:86
  867.9 17.3 %reduce-scatter.2.cloned.1.call-done = f32[8,5280]{1,0:T(8,128)} async-done(((f32[64,5280]{1,0:T(8,128)}), f32[8,5280]{1,0:T(8,128)}) %reduce-scatter.2.cloned.1.call-update) | async-done | bytes 168976 | tf_op jit(solution)/shard_map/reduce_scatter | solution.py:65
  891.7 353.8 %custom-call.11 = f32[8,48,10,10]{3,2,1,0:T(8,128)} custom-call(f32[8,48,10,10]{3,2,1,0:T(8,128)} %broadcast_multiply_fusion), custom_call_target="Cholesky" | custom-call | tf_op jit(solution)/shard_map/jit(cholesky)/cholesky | solution.py:71
  1248.1 9.5 custom-call.12
  1260.4 2.9 convolution_bitcast_fusion
  1263.3 5.1 fusion.25
  (179 shorter events, 55.7 us)
Async XLA Ops:
  7.2 878.1 %reduce-scatter.2.cloned.1.call-start = ((), (), s32[]{:S(2)}) async-start(), calls=%async_computation.2 | async-start | bytes 1548288 | tf_op jit(solution)/shard_map/reduce_scatter | solution.py:65
  8.4 13.6 %collective-permute-start.1 = (f32[12,10,5]{2,1,0:T(8,128)S(1)}, f32[12,10,5]{2,1,0:T(8,128)S(1)}, u32[]{:S(2)}, u32[]{:S(2)}) collective-permute-start(f32[12,10,5]{2,1,0:T(8,128)S(1)} %get-tuple-element.84), channel_id=1, source_target_pairs={{1,0},{2,1},{3,2},{4,3},{5,4},{6,5},{7,6},{9,8},{10,9},{11,10},{12... | collective-permute-start | bytes 7208 | tf_op jit(solution)/shard_map/ppermute | solution.py:17
  9.7 12.4 collective-permute-start
  38.5 4.6 copy-start.29
  266.9 6.9 copy-start.15
  293.7 4.6 copy-start.29
  522.0 6.9 copy-start.15
  548.9 4.6 copy-start.29
  777.2 6.9 copy-start.15
  791.6 7.1 copy-start.16
  791.6 7.1 copy-start.17
  791.7 7.1 copy-start.18
  791.7 7.1 copy-start.19
  791.7 7.1 copy-start.20
  791.7 7.1 copy-start.21
  791.7 7.1 copy-start.22
  791.7 7.1 copy-start.23
  791.7 7.1 copy-start.24
  791.7 7.1 copy-start.25
  791.7 7.1 copy-start.26
  804.6 61.3 %all-to-all-start = ((f32[64,10,512]{2,1,0:T(8,128)}), f32[64,10,512]{2,1,0:T(8,128)S(1)}, u32[]{:S(2)}, u32[]{:S(2)}) async-start(f32[64,10,512]{2,1,0:T(8,128)} %copy.46), calls=%async_computation.1 | async-start | bytes 4194304 | tf_op jit(solution)/shard_map/all_to_all | solution.py:86
  1260.4 9.1 copy-start.14
  1260.4 11.0 copy-start.27
  1260.4 11.0 copy-start.28
  (43 other events, 65.3 us)
Sparse Core Ops, SparseCore 0:
  796.0 89.1 reduce-scatter.1
where the time goes:
time: 1280 us
  matrix products  596 us (47%)
  other arithmetic  462 us (36%)
  waiting for transfers between devices  72.8 us (6%)
  local copies, waits for them, and re-layouts  60.7 us (5%)
  loops' own time  44.9 us (4%)
  blocking collectives  16 us (1%)
  between operations  14.7 us (1%)
    dot_general x3, matrix products, block_terms(): jnp.einsum('szkp,sp->szk', weighted_basis, target, precision=lax.Precisio...  462 us
    another operation x4, other arithmetic, body(): factor = jnp.linalg.cholesky(normal)  354 us
    dot_general x3, matrix products, block_terms(): jnp.einsum('szkp,szlp->szkl', weighted_basis, weighted_basis, precision=l...  121 us
    dot_general x3, other arithmetic, block_terms(): jnp.einsum('szkp,szlp->szkl', weighted_basis, weighted_basis, precision=l...  82.9 us
    all_to_all x1, waiting for transfers between devices, body(): lax.all_to_all(best_basis, 'wave', split_axis=0, concat_axis=2, tiled=True)  55.5 us
    another operation x1, loops' own time, body(): results = lax.map(block_terms, grouped)  44.9 us
  transfers between devices with their start and end apart: 4, of which 2 were waited for; matrix products, arithmetic and copies ran while one was open for 1% of the time, Pallas kernels for 0%

commit v1 on v0

v1 whole, which is shorter than its diff:
```python
import jax
import jax.numpy as jnp
from jax import lax
from jax.experimental import pallas as pl
from jax.experimental.pallas import tpu as pltpu
from jax.sharding import PartitionSpec as P

LANES = 128
BF = jnp.bfloat16

def split(x):
    hi = x.astype(BF)
    lo = (x - hi.astype(jnp.float32)).astype(BF)
    return hi, lo

def band_matrix(r_ref, flux_ref, ivar_ref, wb_ref, a_ref, ae_ref):
    band, S, W = r_ref.shape
    half = band // 2
    wide = W + LANES
    root = jnp.sqrt(ivar_ref[...])
    for d in range(band):
        wb_ref[d] = r_ref[d] * root
    wb_ref[band] = flux_ref[...] * root
    R = 16
    lane = lax.broadcasted_iota(jnp.int32, (R, LANES), 1)
    zero = jnp.zeros((R, LANES), jnp.float32)
    for c in range(S // R):
        rows = pl.ds(c * R, R)
        edge = zero
        for delta in range(band + 1):
            total = None
            taps = range(band - delta) if delta < band else range(band)
            for d in taps:
                other = d + delta if delta < band else band
                term = wb_ref[d, rows, :] * wb_ref[other, rows, :]
                term = jnp.concatenate([term, zero], axis=1)
                shift = (d - half) % wide
                if shift:
                    term = pltpu.roll(term, shift, 1)
                total = term if total is None else total + term
            if delta == 0:
                total = total * 0.5
            hi, lo = split(total[:, :W])
            a_ref[delta, pl.ds(c * R, R), :] = jnp.concatenate([hi, hi], axis=1)
            a_ref[delta, pl.ds(S + c * R, R), :] = jnp.concatenate([lo, lo], axis=1)
            base = 2 * half * delta if delta < band else 0
            back = delta if delta < band else 0
            left = pltpu.roll(total, (base + half) % wide, 1)[:, :LANES]
            right = pltpu.roll(total, (base + half - (W - back)) % wide, 1)[:, :LANES]
            prev = edge if delta < band else zero
            new = jnp.where((lane >= base) & (lane < base + half), left,
                   jnp.where((lane >= base + half) & (lane < base + 2 * half), right, prev))
            if delta < band:
                edge = new
                if delta == band - 1:
                    slot, val = 0, edge
            if delta == band:
                slot, val = 1, new
            if delta >= band - 1:
                hi, lo = split(val)
                ae_ref[slot, pl.ds(c * R, R), :] = hi
                ae_ref[slot, pl.ds(S + c * R, R), :] = lo

def nt(x, w):
    return lax.dot_general(x, w, (((1,), (1,)), ((), ())), preferred_element_type=jnp.float32)

def make_main(K, Z, band, S, W, overlap=True):
    pairs = [(k, l) for k in range(K) for l in range(k, K)]
    NP = len(pairs)
    ZB = 16
    nb = Z // ZB
    half = band // 2
    wide = W + LANES

    def kernel(t_ref, x_ref, r_ref, flux_ref, ivar_ref, out_ref,
               wb_ref, a_ref, ae_ref, s_ref, h_ref, acc_ref):
        band_matrix(r_ref, flux_ref, ivar_ref, wb_ref, a_ref, ae_ref)
        acc_ref[...] = jnp.zeros_like(acc_ref)
        s_ref[:, :, :W] = t_ref[...]
        s_ref[:, :, W:] = jnp.zeros((K, Z, LANES), jnp.float32)

        def build(b, first):
            rows = pl.ds(b * ZB, ZB)
            for q in range(W // LANES):
                lanes = pl.ds(q * LANES, LANES)
                t = [t_ref[k, rows, lanes] for k in range(K)]
                s = [s_ref[k, rows, lanes] for k in range(K)]
                for i, (k, l) in enumerate(pairs):
                    h = t[k] * s[l] + t[l] * s[k]
                    hi, lo = split(h)
                    h_ref[i, rows, lanes] = hi
                    h_ref[i, rows, pl.ds(W + q * LANES, LANES)] = lo

        def shift_s():
            for k in range(K):
                for b in range(Z // 8):
                    rows = pl.ds(b * 8, 8)
                    s_ref[k, rows, :] = pltpu.roll(s_ref[k, rows, :], wide - 1, 1)

        def step(delta, _):
            for b in range(nb):
                build(b, False)
                rows = pl.ds(b * ZB, ZB)
                hb = h_ref[:, rows, :].reshape(NP * ZB, 2 * W)
                acc_ref[:NP, rows, :] += nt(hb, a_ref[delta]).reshape(NP, ZB, 2 * S)
            shift_s()
            return 0
        lax.fori_loop(0, band, step, 0)
        for b in range(nb):
            rows = pl.ds(b * ZB, ZB)
            for k in range(K):
                hi, lo = split(t_ref[k, rows, :])
                h_ref[k, rows, :W] = hi
                h_ref[k, rows, W:] = lo
        hb = h_ref[:K].reshape(K * Z, 2 * W)
        acc_ref[NP:] += nt(hb, a_ref[band]).reshape(K, Z, 2 * S)
        inp = lax.broadcasted_iota(jnp.int32, (LANES, LANES), 0)
        outp = lax.broadcasted_iota(jnp.int32, (LANES, LANES), 1)
        dd = outp // (2 * half)
        ii = outp % (2 * half)
        isl = ii < half
        valid = outp < 2 * half * band
        src1 = jnp.where(isl, ii, 64 + half + ii)
        src2 = jnp.where(isl, ii + dd, 64 + half + ii - dd)
        sel1 = ((inp == src1) & valid).astype(jnp.float32)
        sel2 = ((inp == src2) & valid).astype(jnp.float32)
        x = x_ref[...].reshape(K * Z, LANES)
        hp = lax.Precision.HIGHEST
        e1 = jnp.dot(x, sel1, precision=hp, preferred_element_type=jnp.float32).reshape(K, Z, LANES)
        e2 = jnp.dot(x, sel2, precision=hp, preferred_element_type=jnp.float32).reshape(K, Z, LANES)
        s_ref[:, :, :LANES] = e1
        s_ref[:, :, LANES:2 * LANES] = e2
        for b in range(nb):
            rows = pl.ds(b * ZB, ZB)
            t = [s_ref[k, rows, :LANES] for k in range(K)]
            s = [s_ref[k, rows, LANES:2 * LANES] for k in range(K)]
            for i, (k, l) in enumerate(pairs):
                hi, lo = split(t[k] * s[l] + t[l] * s[k])
                h_ref[i, rows, :LANES] = hi
                h_ref[i, rows, LANES:2 * LANES] = lo
        w = jnp.concatenate([ae_ref[0], ae_ref[0]], axis=1)
        acc_ref[:NP] += nt(h_ref[:NP, :, :2 * LANES].reshape(NP * Z, 2 * LANES), w).reshape(NP, Z, 2 * S)
        for b in range(nb):
            rows = pl.ds(b * ZB, ZB)
            for k in range(K):
                hi, lo = split(s_ref[k, rows, :LANES])
                h_ref[k, rows, :LANES] = hi
                h_ref[k, rows, LANES:2 * LANES] = lo
        w = jnp.concatenate([ae_ref[1], ae_ref[1]], axis=1)
        acc_ref[NP:] += nt(h_ref[:K, :, :2 * LANES].reshape(K * Z, 2 * LANES), w).reshape(K, Z, 2 * S)
        full = acc_ref[...].reshape((NP + K) * Z, 2 * S).T
        out_ref[...] = full[:S] + full[S:]

    n = (NP + K) * Z
    return pl.pallas_call(kernel, out_shape=jax.ShapeDtypeStruct((S, n), jnp.float32),
        scratch_shapes=[pltpu.VMEM((band + 1, S, W), jnp.float32),
                        pltpu.VMEM((band + 1, 2 * S, 2 * W), BF),
                        pltpu.VMEM((2, 2 * S, LANES), BF),
                        pltpu.VMEM((K, Z, wide), jnp.float32),
                        pltpu.VMEM((NP, Z, 2 * W), BF),
                        pltpu.VMEM((NP + K, Z, 2 * S), jnp.float32)],
        compiler_params=pltpu.CompilerParams(vmem_limit_bytes=60 << 20),
        name="normals")


def solve_kernel_for(K, Z, pairs):
    NP = len(pairs)

    def kernel(parts_ref, best_ref, gain_ref, coef_ref):
        n = jnp.sum(parts_ref[...], axis=0)

        def item(i):
            return n[:, i * Z:(i + 1) * Z]
        N = {kl: item(i) for i, kl in enumerate(pairs)}
        proj = [item(NP + k) for k in range(K)]
        L, inv, y = {}, [], []
        for j in range(K):
            for i in range(j, K):
                v = N[(j, i)]
                for m in range(j):
                    v = v - L[(i, m)] * L[(j, m)]
                L[(i, j)] = v
            root = jnp.sqrt(L[(j, j)])
            inv.append(1.0 / root)
            for i in range(j + 1, K):
                L[(i, j)] = L[(i, j)] * inv[j]
            v = proj[j]
            for m in range(j):
                v = v - L[(j, m)] * y[m]
            y.append(v * inv[j])
        c = [None] * K
        for j in reversed(range(K)):
            v = y[j]
            for i in range(j + 1, K):
                v = v - L[(i, j)] * c[i]
            c[j] = v * inv[j]
        chi = proj[0] * c[0]
        for k in range(1, K):
            chi = chi + proj[k] * c[k]
        gain_ref[...] = jnp.log1p(chi / K)
        rows = n.shape[0]
        hit = lax.broadcasted_iota(jnp.int32, (rows, Z), 1) == best_ref[...]
        lane = lax.broadcasted_iota(jnp.int32, (rows, LANES), 1)
        out = jnp.zeros((rows, LANES), jnp.float32)
        for k in range(K):
            v = jnp.sum(jnp.where(hit, c[k], 0.0), axis=1, keepdims=True)
            out = jnp.where(lane == k, v, out)
        coef_ref[...] = out
    return kernel


def model_kernel_for(K, Z, band):
    half = band // 2
    hp = lax.Precision.HIGHEST

    def kernel(t_ref, x_ref, r_ref, coef_ref, best_ref, out_ref):
        S, W = out_ref.shape
        hit = lax.broadcasted_iota(jnp.int32, (S, Z), 1) == best_ref[...]
        main = jnp.zeros((S, W), jnp.float32)
        edge = jnp.zeros((S, LANES), jnp.float32)
        for k in range(K):
            sel = jnp.where(hit, coef_ref[:, k:k + 1], 0.0)
            main = main + jnp.dot(sel, t_ref[k], precision=hp, preferred_element_type=jnp.float32)
            edge = edge + jnp.dot(sel, x_ref[k], precision=hp, preferred_element_type=jnp.float32)
        lane = lax.broadcasted_iota(jnp.int32, (S, LANES), 1)
        right = pltpu.roll(edge, LANES - (64 + 2 * half), 1)
        left = pltpu.roll(edge, LANES - half, 1)
        last = jnp.where(lane < half, right, jnp.where(lane >= LANES - half, left, 0.0))
        u = jnp.concatenate([main, last], axis=1)
        wide = W + LANES
        total = None
        for d in range(band):
            shift = (half - d) % wide
            v = (pltpu.roll(u, shift, 1) if shift else u)[:, :W]
            term = r_ref[d] * v
            total = term if total is None else total + term
        out_ref[...] = total
    return kernel


def body(templates, resolution, coadd_flux, coadd_ivar, best_index, exposures, exposure_mask):
    S, band, W = resolution.shape
    half = band // 2
    K = templates.shape[1]
    nw, ns = lax.axis_size("wave"), lax.axis_size("spec")
    Z = templates.shape[0] * ns
    own = S // nw
    pairs = [(k, l) for k in range(K) for l in range(k, K)]
    columns = (len(pairs) + K) * Z
    up = [(i, i + 1) for i in range(nw - 1)]
    down = [(j, i) for i, j in up]
    before = lax.ppermute(templates[:, :, W - half:], "wave", up)
    after = lax.ppermute(templates[:, :, :half], "wave", down)
    padded = jnp.concatenate([before, templates, after], axis=2)
    full = lax.all_gather(padded, "spec", axis=0, tiled=True)
    full = jnp.transpose(full, (1, 0, 2))
    t = full[:, :, half:half + W]
    x = jnp.concatenate([full[:, :, :3 * half], jnp.zeros((K, Z, 64 - 3 * half), jnp.float32),
                         full[:, :, W - half:], jnp.zeros((K, Z, 64 - 3 * half), jnp.float32)], axis=2)
    r = jnp.transpose(resolution, (1, 0, 2))
    partial = make_main(K, Z, band, S, W)(t, x, r, coadd_flux, coadd_ivar)
    parts = lax.all_to_all(partial.reshape(nw, own, columns), "wave", 0, 0, tiled=True)
    own_best = lax.dynamic_slice_in_dim(best_index, lax.axis_index("wave") * own, own)
    gain, coef = pl.pallas_call(
        solve_kernel_for(K, Z, pairs),
        out_shape=(jax.ShapeDtypeStruct((own, Z), jnp.float32),
                   jax.ShapeDtypeStruct((own, LANES), jnp.float32)),
        name="solve",
    )(parts, own_best[:, None])
    spread = jnp.broadcast_to(coef[None], (nw, own, LANES))
    coefs = lax.all_to_all(spread, "wave", 0, 0, tiled=True).reshape(S, LANES)
    model = pl.pallas_call(
        model_kernel_for(K, Z, band),
        out_shape=jax.ShapeDtypeStruct((S, W), jnp.float32),
        name="model",
    )(t, x, r, coefs, best_index[:, None])
    rows = lax.all_to_all(model.reshape(nw, own, W), "wave", 0, 0, tiled=True)
    rows = jnp.transpose(rows, (1, 0, 2)).reshape(own, 1, nw * W)
    residuals = exposure_mask.astype(jnp.float32) * (exposures - rows)
    return gain, residuals


def solution(mesh):
    in_specs = (
        P("spec", None, "wave"),
        P("spec", None, "wave"),
        P("spec", "wave"),
        P("spec", "wave"),
        P("spec"),
        P(("spec", "wave"), None, None),
        P(("spec", "wave"), None, None),
    )
    out_specs = (P(("spec", "wave"), None), P(("spec", "wave"), None, None))
    return jax.shard_map(body, mesh=mesh, in_specs=in_specs, out_specs=out_specs, check_vma=False)
```

time: 1280 us -> 133 us (0.10)
  matrix products: 596 us -> 0 us
  other arithmetic: 462 us -> 1.97 us
  local copies, waits for them, and re-layouts: 60.7 us -> 7.3 us
  Pallas kernels: 0 us -> 49.4 us
  loops' own time: 44.9 us -> 0 us
  waiting for transfers between devices: 72.8 us -> 31.8 us
  between operations: 14.7 us -> 0.69 us
    dot_general x9 -> x0, matrix products: 588 us -> none  [the longest x3 462 us: block_terms(): jnp.einsum('szkp,sp->szk', weighted_basis, target, precision=lax.Precisio...]
    another operation x7 -> x0, other arithmetic: 364 us -> none  [the longest x4 354 us: body(): factor = jnp.linalg.cholesky(normal)]
    dot_general x3 -> x0, other arithmetic: 82.9 us -> none  [block_terms(): jnp.einsum('szkp,szlp->szkl', weighted_basis, weighted_basis, precision=l...]
    pallas_call x0 -> x3, Pallas kernels: none -> 49.4 us  [the longest x1 40.3 us: body(): partial = make_main(K, Z, band, S, W)(t, x, r, coadd_flux, coadd_ivar)]
    another operation x1 -> x0, loops' own time: 44.9 us -> none  [body(): results = lax.map(block_terms, grouped)]
    all_to_all x1 -> x2, waiting for transfers between devices: 55.5 us -> 26.6 us  [the longest x1 20.6 us: body(): lax.all_to_all(partial.reshape(nw, own, columns), 'wave', 0, 0, tiled=True)]
    dot_general x7 -> x0, local copies, waits for them, and re-layouts: 26.4 us -> none  [the longest x3 20.7 us: block_terms(): jnp.einsum('szkp,szlp->szkl', weighted_basis, weighted_basis, precision=l...]
    reduce_scatter x1 -> x0, waiting for transfers between devices: 17.3 us -> none  [body(): lax.psum_scatter(partials, 'wave', scatter_dimension=0, tiled=True)]
  transfers between devices with their start and end apart: 4 -> 4, of which waited for: 2 -> 4; matrix products, arithmetic and copies ran while one was open for 1% -> 1% of each run, Pallas kernels for 0% -> 0%
where the time goes in v1:
time: 133 us; the launch traced here: 132 us
  Pallas kernels  49.4 us (37%)
  waiting for transfers between devices  31.8 us (24%)
  blocking collectives  25.7 us (19%)
  starting transfers between devices  15.7 us (12%)
  local copies, waits for them, and re-layouts  7.3 us (5%)
  other arithmetic  1.97 us (1%)
    pallas_call x1, Pallas kernels, body(): partial = make_main(K, Z, band, S, W)(t, x, r, coadd_flux, coadd_ivar)  40.3 us
    all_to_all x1, waiting for transfers between devices, body(): lax.all_to_all(partial.reshape(nw, own, columns), 'wave', 0, 0, tiled=True)  20.6 us
    all_gather x1, blocking collectives, body(): full = lax.all_gather(padded, 'spec', axis=0, tiled=True)  15 us
    all_to_all x1, blocking collectives, body(): rows = lax.all_to_all(model.reshape(nw, own, W), 'wave', 0, 0, tiled=True)  10.6 us
    all_to_all x1, waiting for transfers between devices, body(): coefs = lax.all_to_all(spread, 'wave', 0, 0, tiled=True).reshape(S, LANES)  5.99 us
    all_to_all x1, starting transfers between devices, body(): lax.all_to_all(partial.reshape(nw, own, columns), 'wave', 0, 0, tiled=True)  5.88 us
    ppermute x1, starting transfers between devices, body(): before = lax.ppermute(templates[:, :, W - half:], 'wave', up)  4.88 us
    pallas_call x1, Pallas kernels, body(): pl.pallas_call(solve_kernel_for(K, Z, pairs), out_shape=(jax.ShapeDtypeSt...  4.55 us
  transfers between devices with their start and end apart: 4, of which 4 were waited for; matrix products, arithmetic and copies ran while one was open for 1% of the time, Pallas kernels for 0%

profile of v1, /device:TPU:0, one launch (start us, length us, event | category | flops | bytes accessed | tf_op | source)
XLA Modules:
  0.0 132.5 jit_solution(6513681498148504158)
XLA Ops:
  0.6 1.1 copy.11
  1.8 4.9 %collective-permute-start = (f32[12,10,5]{2,1,0:T(8,128)S(1)}, f32[12,10,5]{2,1,0:T(8,128)S(1)}, u32[]{:S(2)}, u32[]{:S(2)}) collective-permute-start(f32[12,10,5]{2,1,0:T(8,128)S(1)} %get-tuple-element.8), channel_id=1, source_target_pairs={{0,1},{1,2},{2,3},{3,4},{4,5},{5,6},{6,7},{8,9},{9,10},{10,11},{11... | collective-permute-start | bytes 7208 | tf_op jit(solution)/shard_map/ppermute | solution.py:252
  6.7 1.3 collective-permute-start.1
  8.0 0.9 collective-permute-done
  8.9 4.3 %collective-permute-done.1 = f32[12,10,5]{2,1,0:T(8,128)S(1)} collective-permute-done((f32[12,10,5]{2,1,0:T(8,128)S(1)}, f32[12,10,5]{2,1,0:T(8,128)S(1)}, u32[]{:S(2)}, u32[]{:S(2)}) %collective-permute-start.1) | collective-permute-done | bytes 2432 | tf_op jit(solution)/shard_map/ppermute | solution.py:253
  13.2 0.2 pad_maximum_fusion
  13.5 15.0 %all_gather.3 = f32[48,10,522]{2,1,0:T(8,128)S(1)} all-gather(f32[12,10,522]{2,1,0:T(8,128)S(1)} %pad_maximum_fusion), channel_id=1, replica_groups=mesh['spec'=4,'wave'=8] {'spec'}, dimensions={0}, use_global_device_ids=true | all-gather | bytes 1252800 | tf_op jit(solution)/shard_map/all_gather | solution.py:255
  28.5 0.4 copy.18
  29.0 1.3 slice.22.t_ref
  30.3 1.0 pad_maximum_fusion.1.x_ref
  31.3 40.3 %normals.1 = f32[64,3120]{1,0:T(8,128)} custom-call(f32[10,48,512]{2,1,0:T(8,128)} %slice.22.t_ref, f32[10,48,128]{2,1,0:T(8,128)} %pad_maximum_fusion.1.x_ref, f32[11,64,512]{2,1,0:T(8,128)} %bitcast.15, f32[64,512]{1,0:T(8,128)} %flux_ref.1, f32[64,512]{1,0:T(8,128)} %ivar_ref.1), custom_call_target="tpu_custom_call" | custom-call | tf_op jit(solution)/shard_map/normals/pallas_call | solution.py:261
  71.6 5.9 %all-to-all-start = ((f32[8,8,3120]{2,1,0:T(8,128)}), f32[8,8,3120]{2,1,0:T(8,128)S(1)}, u32[]{:S(2)}, u32[]{:S(2)}) async-start(f32[8,8,3120]{2,1,0:T(8,128)} %bitcast.17), calls=%async_computation | async-start | bytes 1638400 | tf_op jit(solution)/shard_map/all_to_all | solution.py:262
  77.6 0.7 copy.15.best_ref
  78.2 20.6 %all-to-all-done.parts_ref = f32[8,8,3120]{2,1,0:T(8,128)S(1)} async-done(((f32[8,8,3120]{2,1,0:T(8,128)}), f32[8,8,3120]{2,1,0:T(8,128)S(1)}, u32[]{:S(2)}, u32[]{:S(2)}) %all-to-all-start) | async-done | bytes 798752 | tf_op jit(solution)/shard_map/all_to_all | solution.py:262
  98.9 0.9 copy-done
  99.8 4.5 %solve.1 = (f32[8,48]{1,0:T(8,128)}, f32[8,128]{1,0:T(8,128)}) custom-call(f32[8,8,3120]{2,1,0:T(8,128)} %copy-done, s32[8,1]{1,0:T(8,128)} %copy.15.best_ref), custom_call_target="tpu_custom_call" | custom-call | tf_op jit(solution)/shard_map/solve/pallas_call | solution.py:264
  104.4 1.3 broadcast_in_dim.13
  105.7 3.6 %all-to-all-start.1 = ((f32[8,8,128]{2,1,0:T(8,128)}), f32[8,8,128]{2,1,0:T(8,128)S(1)}, u32[]{:S(2)}, u32[]{:S(2)}) async-start(f32[8,8,128]{2,1,0:T(8,128)} %broadcast_in_dim.13), calls=%async_computation.1 | async-start | bytes 65536 | tf_op jit(solution)/shard_map/all_to_all | solution.py:271
  109.3 0.7 copy.16.best_ref
  110.0 6.0 %all-to-all-done.1 = f32[8,8,128]{2,1,0:T(8,128)S(1)} async-done(((f32[8,8,128]{2,1,0:T(8,128)}), f32[8,8,128]{2,1,0:T(8,128)S(1)}, u32[]{:S(2)}, u32[]{:S(2)}) %all-to-all-start.1) | async-done | bytes 32800 | tf_op jit(solution)/shard_map/all_to_all | solution.py:271
  116.0 0.6 copy-done.3
  116.6 4.5 %model.1 = f32[64,512]{1,0:T(8,128)} custom-call(f32[10,48,512]{2,1,0:T(8,128)} %slice.22.t_ref, f32[10,48,128]{2,1,0:T(8,128)} %pad_maximum_fusion.1.x_ref, f32[11,64,512]{2,1,0:T(8,128)} %bitcast.16, f32[64,128]{1,0:T(8,128)} %bitcast.20, s32[64,1]{1,0:T(8,128)} %copy.16.best_ref), custom_call_target="tpu_custom_call" | custom-call | tf_op jit(solution)/shard_map/model/pallas_call | solution.py:272
  121.1 10.6 %all_to_all.15 = f32[8,8,512]{2,1,0:T(8,128)S(1)} all-to-all(f32[8,8,512]{2,1,0:T(8,128)} %bitcast.18), channel_id=1, replica_groups=mesh['spec'=4,'wave'=8] {'wave'}, dimensions={0} | all-to-all | bytes 262144 | tf_op jit(solution)/shard_map/all_to_all | solution.py:277
  131.7 0.8 subtract_multiply_fusion
  (12 shorter events, 0.3 us)
Async XLA Ops:
  1.8 7.1 %collective-permute-start = (f32[12,10,5]{2,1,0:T(8,128)S(1)}, f32[12,10,5]{2,1,0:T(8,128)S(1)}, u32[]{:S(2)}, u32[]{:S(2)}) collective-permute-start(f32[12,10,5]{2,1,0:T(8,128)S(1)} %get-tuple-element.8), channel_id=1, source_target_pairs={{0,1},{1,2},{2,3},{3,4},{4,5},{5,6},{6,7},{8,9},{9,10},{10,11},{11... | collective-permute-start | bytes 7208 | tf_op jit(solution)/shard_map/ppermute | solution.py:252
  6.7 6.5 %collective-permute-start.1 = (f32[12,10,5]{2,1,0:T(8,128)S(1)}, f32[12,10,5]{2,1,0:T(8,128)S(1)}, u32[]{:S(2)}, u32[]{:S(2)}) collective-permute-start(f32[12,10,5]{2,1,0:T(8,128)S(1)} %get-tuple-element.9), channel_id=1, source_target_pairs={{1,0},{2,1},{3,2},{4,3},{5,4},{6,5},{7,6},{9,8},{10,9},{11,10},{12... | collective-permute-start | bytes 7208 | tf_op jit(solution)/shard_map/ppermute | solution.py:253
  71.6 5.9 %copy-start.4 = (s32[64]{0:T(128)S(1)}, s32[64]{0:T(128)}, u32[]{:S(2)}) copy-start(s32[64]{0:T(128)} %param.11) | copy-start | bytes 772
  71.6 27.3 %all-to-all-start = ((f32[8,8,3120]{2,1,0:T(8,128)}), f32[8,8,3120]{2,1,0:T(8,128)S(1)}, u32[]{:S(2)}, u32[]{:S(2)}) async-start(f32[8,8,3120]{2,1,0:T(8,128)} %bitcast.17), calls=%async_computation | async-start | bytes 1638400 | tf_op jit(solution)/shard_map/all_to_all | solution.py:262
  98.9 0.9 copy-start
  105.7 10.3 %all-to-all-start.1 = ((f32[8,8,128]{2,1,0:T(8,128)}), f32[8,8,128]{2,1,0:T(8,128)S(1)}, u32[]{:S(2)}, u32[]{:S(2)}) async-start(f32[8,8,128]{2,1,0:T(8,128)} %broadcast_in_dim.13), calls=%async_computation.1 | async-start | bytes 65536 | tf_op jit(solution)/shard_map/all_to_all | solution.py:271
  116.0 0.6 copy-start.3
  116.6 15.1 %copy-start.1 = (f32[8,3,4096]{2,0,1:T(8,128)S(1)}, f32[8,3,4096]{2,0,1:T(8,128)}, u32[]{:S(2)}) copy-start(f32[8,3,4096]{2,0,1:T(8,128)} %param.12) | copy-start | bytes 1179652
  116.6 15.1 %copy-start.2 = (s32[8,3,4096]{2,0,1:T(8,128)S(1)}, s32[8,3,4096]{2,0,1:T(8,128)}, u32[]{:S(2)}) copy-start(s32[8,3,4096]{2,0,1:T(8,128)} %param.13) | copy-start | bytes 1179652

commit v2 on v0

v2 whole, which is shorter than its diff:
```python
import jax
import jax.numpy as jnp
from jax import lax
from jax.experimental import pallas as pl
from jax.experimental.pallas import tpu as pltpu
from jax.sharding import PartitionSpec as P


LANES = 128
BF = jnp.bfloat16


def split(x):
    hi = x.astype(BF)
    return hi, (x - hi.astype(jnp.float32)).astype(BF)


def dot(x, w):
    return jnp.dot(x, w, preferred_element_type=jnp.float32)


def pair_list(K):
    return [(k, l) for k in range(K) for l in range(k, K)]


def put(h_ref, row, q, width, a, c):
    hi, lo = split(jnp.concatenate([a, c], axis=0))
    h_ref[row, :, q * LANES:(q + 1) * LANES] = hi
    h_ref[row, :, width + q * LANES:width + (q + 1) * LANES] = lo


def pair_block(h_ref, t, s, b, blocks, q, width):
    pairs = pair_list(len(t))
    items = [t[k] * s[l] + t[l] * s[k] for k, l in pairs]
    items += [jnp.zeros_like(t[0])] * (len(pairs) % 2)
    for i in range(len(items) // 2):
        put(h_ref, i * blocks + b, q, width, items[2 * i], items[2 * i + 1])


def single_block(h_ref, t, b, blocks, q, width):
    items = t + [jnp.zeros_like(t[0])] * (len(t) % 2)
    for i in range(len(items) // 2):
        put(h_ref, i * blocks + b, q, width, items[2 * i], items[2 * i + 1])


def make_main(K, Z, band, S, W):
    pairs = pair_list(K)
    NP = len(pairs)
    NQ = (NP + 1) // 2
    KQ = (K + 1) // 2
    ZB = Z // 8
    half = band // 2
    wide = W + LANES
    top = 24
    N = 2 * S
    step = 16

    def band_matrix(own_ref, other_ref, wb_ref, a_ref, rhs_ref, edge_ref, aeb_ref):
        root_own = jnp.sqrt(own_ref[band])
        root_other = jnp.sqrt(other_ref[band])
        zero = jnp.zeros((band + 1, top, N), jnp.float32)
        wb_ref[:, :top, :] = zero
        wb_ref[:, top + W:, :] = zero
        for d in range(band + 1):
            src = d if d < band else band + 1
            both = jnp.concatenate([own_ref[src] * root_own, other_ref[src] * root_other], axis=0)
            wb_ref[d, top:top + W, :] = both.T

        def block(i, _):
            base = pl.multiple_of(i * step, step)
            for part in range(step // 8):
                acc = [None] * (band + 1)
                for d in range(band):
                    rows = pl.ds(base + (part * 8 + top - step + half - d), 8)
                    v = [wb_ref[e, rows, :] for e in range(d, band + 1)]
                    for e in range(d, band + 1):
                        o = e - d if e < band else band
                        p = v[0] * v[e - d]
                        acc[o] = p if acc[o] is None else acc[o] + p
                acc[0] = acc[0] * 0.5
                for o in range(band + 1):
                    a_ref[o, pl.ds(base + part * 8, 8), :] = acc[o]
            for o in range(band + 1):
                hi, lo = split(a_ref[o, pl.ds(base, step), :])
                rhs_ref[o, pl.ds(base, step), :N] = hi
                rhs_ref[o, pl.ds(base, step), N:] = lo
            return 0

        lax.fori_loop(0, (W + 2 * step) // step, block, 0)
        edge_ref[...] = jnp.zeros_like(edge_ref)
        for o in range(band):
            edge_ref[0, 2 * half * o:2 * half * o + half, :] = a_ref[o, step - half:step, :]
            edge_ref[0, 2 * half * o + half:2 * half * (o + 1), :] = a_ref[o, step + W - o:step + W - o + half, :]
        edge_ref[1, :half, :] = a_ref[band, step - half:step, :]
        edge_ref[1, half:2 * half, :] = a_ref[band, step + W:step + W + half, :]
        for o in range(2):
            hi, lo = split(edge_ref[o])
            aeb_ref[o, :, :N] = hi
            aeb_ref[o, :, N:] = lo

    def kernel(t_ref, own_ref, other_ref, out_ref, aeb_ref,
               wb_ref, a_ref, rhs_ref, edge_ref, s_ref, h0_ref, h1_ref, acc_ref):
        band_matrix(own_ref, other_ref, wb_ref, a_ref, rhs_ref, edge_ref, aeb_ref)
        s_ref[:, :, :W] = t_ref[...]
        s_ref[:, :, W:] = jnp.zeros((K, Z, LANES), jnp.float32)
        acc_ref[...] = jnp.zeros_like(acc_ref)

        def build(h_ref):
            for b in range(ZB):
                rows = pl.ds(b * 8, 8)
                for q in range(W // LANES):
                    lanes = pl.ds(q * LANES, LANES)
                    t = [t_ref[k, rows, lanes] for k in range(K)]
                    s = [s_ref[k, rows, lanes] for k in range(K)]
                    pair_block(h_ref, t, s, b, ZB, q, W)

        def advance():
            for k in range(K):
                for b in range(ZB):
                    rows = pl.ds(b * 8, 8)
                    s_ref[k, rows, :] = pltpu.roll(s_ref[k, rows, :], wide - 1, 1)

        def add(h_ref, first, count, width, w):
            h = h_ref[:count, :, :2 * width].reshape(count * 16, 2 * width)
            v = dot(h[:, :width], w) + dot(h[:, width:], w)
            acc_ref[first:first + count] += v.reshape(count, 16, 2 * N)

        def weights(o):
            return rhs_ref[o, step:step + W, :]

        build(h0_ref)
        advance()

        def pair_step(i, _):
            build(h1_ref)
            advance()
            add(h0_ref, 0, NQ * ZB, W, weights(2 * i))
            build(h0_ref)
            advance()
            add(h1_ref, 0, NQ * ZB, W, weights(2 * i + 1))
            return 0

        lax.fori_loop(0, band // 2, pair_step, 0)
        for b in range(ZB):
            rows = pl.ds(b * 8, 8)
            for q in range(W // LANES):
                single_block(h1_ref, [t_ref[k, rows, pl.ds(q * LANES, LANES)] for k in range(K)], b, ZB, q, W)
        add(h0_ref, 0, NQ * ZB, W, weights(band - 1))
        add(h1_ref, NQ * ZB, KQ * ZB, W, weights(band))
        acc = acc_ref[:, :, :N] + acc_ref[:, :, N:]
        out_ref[...] = acc.reshape((NQ + KQ) * ZB * 16, N)

    return pl.pallas_call(
        kernel,
        out_shape=(jax.ShapeDtypeStruct(((NQ + KQ) * ZB * 16, N), jnp.float32),
                   jax.ShapeDtypeStruct((2, LANES, 2 * N), BF)),
        scratch_shapes=[pltpu.VMEM((band + 1, W + 2 * top, N), jnp.float32),
                        pltpu.VMEM((band + 1, W + 2 * step, N), jnp.float32),
                        pltpu.VMEM((band + 1, W + 2 * step, 2 * N), BF),
                        pltpu.VMEM((2, LANES, N), jnp.float32),
                        pltpu.VMEM((K, Z, wide), jnp.float32),
                        pltpu.VMEM((NQ * ZB, 16, 2 * W), BF),
                        pltpu.VMEM((NQ * ZB, 16, 2 * W), BF),
                        pltpu.VMEM(((NQ + KQ) * ZB, 16, 2 * N), jnp.float32)],
        compiler_params=pltpu.CompilerParams(vmem_limit_bytes=60 << 20),
        name="normals")


def make_edge(K, Z, band, S, planes, own):
    NP = K * (K + 1) // 2
    NQ, KQ, ZB = (NP + 1) // 2, (K + 1) // 2, Z // 8
    half = band // 2
    N = 2 * S
    hp = lax.Precision.HIGHEST

    def kernel(acc_ref, aeb_ref, x_ref, own_ref, other_ref, out_ref, nb_ref, nb2_ref, h_ref):
        inp = lax.broadcasted_iota(jnp.int32, (LANES, LANES), 0)
        outp = lax.broadcasted_iota(jnp.int32, (LANES, LANES), 1)
        dd = outp // (2 * half)
        ii = outp % (2 * half)
        isl = ii < half
        valid = outp < 2 * half * band
        src1 = jnp.where(isl, ii, 64 + half + ii)
        src2 = jnp.where(isl, ii + dd, 64 + half + ii - dd)
        sel1 = ((inp == src1) & valid).astype(jnp.float32)
        sel2 = ((inp == src2) & valid).astype(jnp.float32)
        x = x_ref[...].reshape(K * Z, LANES)
        e1 = jnp.dot(x, sel1, precision=hp, preferred_element_type=jnp.float32).reshape(K, Z, LANES)
        e2 = jnp.dot(x, sel2, precision=hp, preferred_element_type=jnp.float32).reshape(K, Z, LANES)
        for b in range(ZB):
            t = [e1[k, b * 8:(b + 1) * 8] for k in range(K)]
            s = [e2[k, b * 8:(b + 1) * 8] for k in range(K)]
            pair_block(h_ref, t, s, b, ZB, 0, LANES)
            single_block(h_ref.at[NQ * ZB:], t, b, ZB, 0, LANES)
        h = h_ref[...].reshape((NQ + KQ) * ZB * 16, 2 * LANES)
        cut = NQ * ZB * 16
        sums = []
        for part, o in ((h[:cut], 0), (h[cut:], 1)):
            v = dot(part[:, :LANES], aeb_ref[o]) + dot(part[:, LANES:], aeb_ref[o])
            sums.append(v[:, :N] + v[:, N:])
        acc = acc_ref[...] + jnp.concatenate(sums, axis=0)
        acc = acc.reshape(NQ + KQ, ZB, 2, 8, N)
        place = jnp.concatenate([own_ref[0], other_ref[0]], axis=0).T[:1, :]
        zrow = lax.broadcasted_iota(jnp.int32, (Z, N), 0).astype(jnp.float32)
        hit = zrow == place
        nb_ref[...] = jnp.zeros_like(nb_ref)
        nb2_ref[...] = jnp.zeros_like(nb2_ref)
        parts = []
        for n in range(NP + K):
            i, par = (n // 2, n % 2) if n < NP else (NQ + (n - NP) // 2, (n - NP) % 2)
            item = jnp.concatenate([acc[i, b, par] for b in range(ZB)], axis=0)
            parts.append(item)
            best = jnp.sum(jnp.where(hit, item, 0.0), axis=0, keepdims=True)
            at = (n // 8) * LANES
            nb_ref[n % 8:n % 8 + 1, at:at + S] = best[:, :S]
            nb2_ref[n % 8:n % 8 + 1, at:at + S] = best[:, S:]
        full = jnp.concatenate(parts, axis=0).T
        for w in range(S // own):
            out_ref[2 * own * w:2 * own * w + own] = full[own * w:own * (w + 1)]
            out_ref[2 * own * w + own:2 * own * (w + 1)] = full[S + own * w:S + own * (w + 1)]

    n = (NP + K) * Z

    def whole(*shape):
        return pl.BlockSpec(shape, lambda i: (0,) * len(shape))

    rows = (NQ + KQ) * ZB * 16
    return pl.pallas_call(
        kernel, grid=(1,),
        out_shape=(jax.ShapeDtypeStruct((N, n), jnp.float32),) + (jax.ShapeDtypeStruct((8, n), jnp.float32),) * 2,
        out_specs=(whole(N, n), whole(8, n), whole(8, n)),
        in_specs=[whole(rows, N), whole(2, LANES, 2 * N), whole(K, Z, LANES),
                  pl.BlockSpec((1, S, LANES), lambda i: (planes - 1, 0, 0)),
                  pl.BlockSpec((1, S, LANES), lambda i: (planes - 1, 0, 1))],
        scratch_shapes=[pltpu.VMEM(((NQ + KQ) * ZB, 16, 2 * LANES), BF)],
        compiler_params=pltpu.CompilerParams(vmem_limit_bytes=60 << 20),
        name="edges")


def factor_solve(N, proj):
    K = len(proj)
    L, inv, y = {}, [], []
    for j in range(K):
        for i in range(j, K):
            v = N[(j, i)]
            for m in range(j):
                v = v - L[(i, m)] * L[(j, m)]
            L[(i, j)] = v
        inv.append(1.0 / jnp.sqrt(L[(j, j)]))
        for i in range(j + 1, K):
            L[(i, j)] = L[(i, j)] * inv[j]
        v = proj[j]
        for m in range(j):
            v = v - L[(j, m)] * y[m]
        y.append(v * inv[j])
    c = [None] * K
    for j in reversed(range(K)):
        v = y[j]
        for i in range(j + 1, K):
            v = v - L[(i, j)] * c[i]
        c[j] = v * inv[j]
    return c


def fit_kernel_for(K, Z):
    pairs = pair_list(K)
    NP = len(pairs)

    def kernel(n_ref, gain_ref):
        n = n_ref[...]
        proj = [n[:, (NP + k) * Z:(NP + k + 1) * Z] for k in range(K)]
        c = factor_solve({kl: n[:, i * Z:(i + 1) * Z] for i, kl in enumerate(pairs)}, proj)
        chi = proj[0] * c[0]
        for k in range(1, K):
            chi = chi + proj[k] * c[k]
        gain_ref[...] = jnp.log1p(chi / K)

    return kernel


def model_kernel_for(K, Z, band):
    pairs = pair_list(K)
    NP = len(pairs)
    half = band // 2
    hp = lax.Precision.HIGHEST

    def kernel(nb_ref, t_ref, x_ref, t2_ref, x2_ref, pack_ref, model_ref):
        S, W = model_ref.shape

        def best(n):
            at = (n // 8) * LANES
            return nb_ref[n % 8:n % 8 + 1, at:at + S]

        c = factor_solve({kl: best(i) for i, kl in enumerate(pairs)}, [best(NP + k) for k in range(K)])
        pad = jnp.zeros((LANES - K, S), jnp.float32)
        coef = jnp.concatenate(c + [pad], axis=0).T
        place = pack_ref[band + 2, :, :1]
        lane = lax.broadcasted_iota(jnp.int32, (S, K * Z), 1)
        cols = jnp.zeros((S, K * Z), jnp.float32)
        for k in range(K):
            cols = jnp.where(lane // Z == k, coef[:, k:k + 1], cols)
        main, edge = None, None
        for part, (a_ref, b_ref) in enumerate(((t_ref, x_ref), (t2_ref, x2_ref))):
            sel = jnp.where((lane % Z + part * Z).astype(jnp.float32) == place, cols, 0.0)
            m = jnp.dot(sel, a_ref[...].reshape(K * Z, W), precision=hp, preferred_element_type=jnp.float32)
            e = jnp.dot(sel, b_ref[...].reshape(K * Z, LANES), precision=hp, preferred_element_type=jnp.float32)
            main = m if main is None else main + m
            edge = e if edge is None else edge + e
        lane = lax.broadcasted_iota(jnp.int32, (S, LANES), 1)
        right = pltpu.roll(edge, LANES - (64 + 2 * half), 1)
        left = pltpu.roll(edge, LANES - half, 1)
        last = jnp.where(lane < half, right, jnp.where(lane >= LANES - half, left, 0.0))
        u = jnp.concatenate([main, last], axis=1)
        wide = W + LANES
        total = None
        for d in range(band):
            shift = (half - d) % wide
            v = (pltpu.roll(u, shift, 1) if shift else u)[:, :W]
            term = pack_ref[d] * v
            total = term if total is None else total + term
        model_ref[...] = total

    return kernel


def body(templates, resolution, coadd_flux, coadd_ivar, best_index, exposures, exposure_mask):
    S, band, W = resolution.shape
    half = band // 2
    zo, K, _ = templates.shape
    nw, ns = lax.axis_size("wave"), lax.axis_size("spec")
    Z = zo * ns // 2
    own = S // nw
    me, wave = lax.axis_index("spec"), lax.axis_index("wave")

    def swap(x, axis, m):
        return lax.ppermute(x, axis, [(i, i ^ m) for i in range(lax.axis_size(axis))])

    def place_for(index):
        rel = (best_index // zo) ^ index
        return ((rel % 2) * Z + (rel // 2) * zo + best_index % zo).astype(jnp.float32)

    where_lane = jnp.arange(W, dtype=jnp.int32)[None, :] < LANES
    plane = jnp.where(where_lane, place_for(me)[:, None], place_for(me ^ 1)[:, None])
    pack = jnp.concatenate([jnp.transpose(resolution, (1, 0, 2)), coadd_ivar[None], coadd_flux[None], plane[None]], axis=0)
    block = jnp.transpose(templates, (1, 0, 2))
    blocks = [block] + [swap(block, "spec", m) for m in range(2, ns, 2)]
    other_pack = swap(pack, "spec", 1)
    ends = jnp.concatenate([block[:, :, W - half:], block[:, :, :half]], axis=2)
    ends = jnp.concatenate([ends] + [swap(ends, "spec", m) for m in range(2, ns, 2)], axis=1)
    up = [(i, i + 1) for i in range(nw - 1)]
    before = lax.ppermute(ends[:, :, :half], "wave", up)
    after = lax.ppermute(ends[:, :, half:], "wave", [(j, i) for i, j in up])
    t = jnp.concatenate(blocks, axis=1)
    acc, aeb = make_main(K, Z, band, S, W)(t, pack, other_pack)
    acc, before, after = lax.optimization_barrier((acc, before, after))
    gap = jnp.zeros((K, Z, 64 - 3 * half), jnp.float32)
    x = jnp.concatenate([before, t[:, :, :2 * half], gap, t[:, :, W - 2 * half:], after, gap], axis=2)
    t2, x2 = swap(t, "spec", 1), swap(x, "spec", 1)
    d, nb, nb2 = make_edge(K, Z, band, S, band + 3, own)(acc, aeb, x, pack, other_pack)
    columns = d.shape[1]
    d = d.reshape(nw, 2 * own, columns)
    bit = 1
    while bit < nw:
        d = d.reshape(d.shape[0] // 2, 2, 2 * own, columns)
        b = (wave // bit) % 2
        keep = lax.dynamic_index_in_dim(d, b, 1, keepdims=False)
        send = lax.dynamic_index_in_dim(d, 1 - b, 1, keepdims=False).reshape(-1, columns)
        if bit == 1:
            d = keep + swap(send, "wave", bit).reshape(keep.shape)
            nb = nb + swap(nb2, "spec", 1)
            nb = nb + swap(nb, "wave", bit)
        else:
            got = swap(jnp.concatenate([send, nb], axis=0), "wave", bit)
            d = keep + got[:-8].reshape(keep.shape)
            nb = nb + got[-8:]
        bit *= 2
    model = pl.pallas_call(
        model_kernel_for(K, Z, band), out_shape=jax.ShapeDtypeStruct((S, W), jnp.float32),
        compiler_params=pltpu.CompilerParams(vmem_limit_bytes=60 << 20), name="model",
    )(nb, t, x, t2, x2, pack)
    rows = lax.all_to_all(model.reshape(nw, own, W), "wave", 0, 0, tiled=True)
    gain = pl.pallas_call(
        fit_kernel_for(K, Z), out_shape=jax.ShapeDtypeStruct((2 * own, Z), jnp.float32), name="fit",
    )(d[0])
    halves = jnp.stack([gain[:own], swap(gain[own:], "spec", 1)], axis=0).reshape(2, own, ns // 2, zo)
    gain = jnp.transpose(halves, (1, 2, 0, 3)).reshape(own, ns, zo)
    bit = 1
    while bit < ns:
        flipped = gain.reshape(own, ns // (2 * bit), 2, bit, zo)[:, :, ::-1].reshape(own, ns, zo)
        gain = jnp.where((me // bit) % 2 == 1, flipped, gain)
        bit *= 2
    gain = gain.reshape(own, ns * zo)
    rows = jnp.transpose(rows, (1, 0, 2)).reshape(own, 1, nw * W)
    residuals = exposure_mask.astype(jnp.float32) * (exposures - rows)
    return gain, residuals


def solution(mesh):
    in_specs = (
        P("spec", None, "wave"),
        P("spec", None, "wave"),
        P("spec", "wave"),
        P("spec", "wave"),
        P("spec"),
        P(("spec", "wave"), None, None),
        P(("spec", "wave"), None, None),
    )
    out_specs = (P(("spec", "wave"), None), P(("spec", "wave"), None, None))
    return jax.shard_map(body, mesh=mesh, in_specs=in_specs, out_specs=out_specs, check_vma=False)
```

time: 1280 us -> 99.7 us (0.08)
  matrix products: 596 us -> 0 us
  other arithmetic: 462 us -> 7.42 us
  local copies, waits for them, and re-layouts: 60.7 us -> 5.33 us
  loops' own time: 44.9 us -> 0 us
  waiting for transfers between devices: 72.8 us -> 31.7 us
  Pallas kernels: 0 us -> 32.7 us
  blocking collectives: 16 us -> 0 us
  between operations: 14.7 us -> 0.88 us
    dot_general x9 -> x0, matrix products: 588 us -> none  [the longest x3 462 us: block_terms(): jnp.einsum('szkp,sp->szk', weighted_basis, target, precision=lax.Precisio...]
    another operation x7 -> x0, other arithmetic: 364 us -> none  [the longest x4 354 us: body(): factor = jnp.linalg.cholesky(normal)]
    dot_general x3 -> x0, other arithmetic: 82.9 us -> none  [block_terms(): jnp.einsum('szkp,szlp->szkl', weighted_basis, weighted_basis, precision=l...]
    all_to_all x1, waiting for transfers between devices: 55.5 us -> 6.7 us  [body(): rows = lax.all_to_all(model.reshape(nw, own, W), 'wave', 0, 0, tiled=True)]
    another operation x1 -> x0, loops' own time: 44.9 us -> none  [body(): results = lax.map(block_terms, grouped)]
    pallas_call x0 -> x4, Pallas kernels: none -> 32.7 us  [the longest x1 20.6 us: body(): acc, aeb = make_main(K, Z, band, S, W)(t, pack, other_pack)]
    dot_general x7 -> x0, local copies, waits for them, and re-layouts: 26.4 us -> none  [the longest x3 20.7 us: block_terms(): jnp.einsum('szkp,szlp->szkl', weighted_basis, weighted_basis, precision=l...]
    ppermute x2 -> x13, waiting for transfers between devices: 0.01 us -> 25 us  [the longest x11 25 us: swap(): lax.ppermute(x, axis, [(i, i ^ m) for i in range(lax.axis_size(axis))])]
  transfers between devices with their start and end apart: 4 -> 14, of which waited for: 2 -> 7; matrix products, arithmetic and copies ran while one was open for 1% -> 5% of each run, Pallas kernels for 0% -> 30%
where the time goes in v2:
time: 99.7 us; the launch traced here: 99.2 us
  Pallas kernels  32.7 us (33%)
  waiting for transfers between devices  31.7 us (32%)
  starting transfers between devices  21.2 us (21%)
  other arithmetic  7.42 us (7%)
  local copies, waits for them, and re-layouts  5.33 us (5%)
    ppermute x11, waiting for transfers between devices, swap(): lax.ppermute(x, axis, [(i, i ^ m) for i in range(lax.axis_size(axis))])  25 us
    pallas_call x1, Pallas kernels, body(): acc, aeb = make_main(K, Z, band, S, W)(t, pack, other_pack)  20.6 us
    ppermute x11, starting transfers between devices, swap(): lax.ppermute(x, axis, [(i, i ^ m) for i in range(lax.axis_size(axis))])  10.1 us
    all_to_all x1, waiting for transfers between devices, body(): rows = lax.all_to_all(model.reshape(nw, own, W), 'wave', 0, 0, tiled=True)  6.7 us
    all_to_all x1, starting transfers between devices, body(): rows = lax.all_to_all(model.reshape(nw, own, W), 'wave', 0, 0, tiled=True)  5.88 us
    pallas_call x1, Pallas kernels, body(): pl.pallas_call(fit_kernel_for(K, Z), out_shape=jax.ShapeDtypeStruct((2 *...  4.57 us
    pallas_call x1, Pallas kernels, body(): pl.pallas_call(model_kernel_for(K, Z, band), out_shape=jax.ShapeDtypeStru...  4.27 us
    ppermute x1, starting transfers between devices, body(): before = lax.ppermute(ends[:, :, :half], 'wave', up)  3.9 us
  transfers between devices with their start and end apart: 14, of which 7 were waited for; matrix products, arithmetic and copies ran while one was open for 5% of the time, Pallas kernels for 30%

profile of v2, /device:TPU:0, one launch (start us, length us, event | category | flops | bytes accessed | tf_op | source)
XLA Modules:
  0.0 99.2 jit_solution(13081118207062619770)
XLA Ops:
  2.1 1.8 %pad_maximum_fusion.own_ref.pack_ref = f32[14,64,512]{2,1,0:T(8,128)S(1)} fusion(f32[1,64,512]{2,1,0:T(8,128)S(1)} %broadcast_select_fusion, f32[1,64,512]{2,1,0:T(8,128)} %bitcast.39, f32[1,64,512]{2,1,0:T(8,128)} %bitcast.40, f32[11,64,512]{2,1,0:T(8,128)} %bitcast.31), kind=kLoop, calls=%fused_computation | loop fusion | flops 1376256 | bytes 3670016 | tf_op jit(solution)/shard_map/concatenate | solution.py:344
  4.6 2.6 %collective-permute-start.2 = (f32[10,12,10]{2,1,0:T(8,128)S(1)}, f32[10,12,10]{2,1,0:T(8,128)S(1)}, u32[]{:S(2)}, u32[]{:S(2)}) collective-permute-start(f32[10,12,10]{2,1,0:T(8,128)S(1)} %pad_maximum_fusion.5), channel_id=1, source_target_pairs={{0,16},{8,24},{16,0},{24,8},{1,17},{9,25},{17,1},{25,9},{2,18},{10... | collective-permute-start | bytes 14408 | tf_op jit(solution)/shard_map/ppermute | solution.py:336
  7.3 3.2 %collective-permute-done.2 = f32[10,12,10]{2,1,0:T(8,128)S(1)} collective-permute-done((f32[10,12,10]{2,1,0:T(8,128)S(1)}, f32[10,12,10]{2,1,0:T(8,128)S(1)}, u32[]{:S(2)}, u32[]{:S(2)}) %collective-permute-start.2) | collective-permute-done | bytes 4832 | tf_op jit(solution)/shard_map/ppermute | solution.py:336
  10.7 3.9 %collective-permute-start.3 = (f32[10,24,5]{2,1,0:T(8,128)S(1)}, f32[10,24,5]{2,1,0:T(8,128)S(1)}, u32[]{:S(2)}, u32[]{:S(2)}) collective-permute-start(f32[10,24,5]{2,1,0:T(8,128)S(1)} %get-tuple-element.27), channel_id=1, source_target_pairs={{0,1},{1,2},{2,3},{3,4},{4,5},{5,6},{6,7},{8,9},{9,10},{10,11},{11... | collective-permute-start | bytes 14408 | tf_op jit(solution)/shard_map/ppermute | solution.py:351
  14.6 1.3 %collective-permute-start.4 = (f32[10,24,5]{2,1,0:T(8,128)S(1)}, f32[10,24,5]{2,1,0:T(8,128)S(1)}, u32[]{:S(2)}, u32[]{:S(2)}) collective-permute-start(f32[10,24,5]{2,1,0:T(8,128)S(1)} %get-tuple-element.26), channel_id=1, source_target_pairs={{1,0},{2,1},{3,2},{4,3},{5,4},{6,5},{7,6},{9,8},{10,9},{11,10},{12... | collective-permute-start | bytes 14408 | tf_op jit(solution)/shard_map/ppermute | solution.py:352
  15.9 1.4 %collective-permute-done = f32[10,12,512]{2,1,0:T(8,128)S(1)} collective-permute-done((f32[10,12,512]{2,1,0:T(8,128)S(1)}, f32[10,12,512]{2,1,0:T(8,128)S(1)}, u32[]{:S(2)}, u32[]{:S(2)}) %collective-permute-start) | collective-permute-done | bytes 245792 | tf_op jit(solution)/shard_map/ppermute | solution.py:336
  17.4 0.8 pad_maximum_fusion.1.t_ref
  18.3 20.6 %normals.1 = (f32[1584,128]{1,0:T(8,128)}, bf16[2,128,256]{2,1,0:T(8,128)(2,1)}) custom-call(f32[10,24,512]{2,1,0:T(8,128)} %pad_maximum_fusion.1.t_ref, f32[14,64,512]{2,1,0:T(8,128)} %copy-done, f32[14,64,512]{2,1,0:T(8,128)} %collective-permute-done.1.other_ref), custom_call_target="tpu_custom_call" | custom-call | tf_op jit(solution)/shard_map/normals/pallas_call | solution.py:354
  38.9 0.9 concatenate.26.x_ref
  39.8 3.3 %edges.1 = (f32[128,1560]{1,0:T(8,128)}, f32[8,1560]{1,0:T(8,128)}, f32[8,1560]{1,0:T(8,128)}) custom-call(f32[1584,128]{1,0:T(8,128)} %get-tuple-element.11.acc_ref, bf16[2,128,256]{2,1,0:T(8,128)(2,1)} %get-tuple-element.12.aeb_ref, f32[10,24,128]{2,1,0:T(8,128)} %concatenate.26.x_ref, f32[14,64,512]{2,1,0:T(8,128)} %copy-done, ...), custom_call_target="tpu_custom_call" | custom-call | tf_op jit(solution)/shard_map/edges/pallas_call | solution.py:359
  43.1 1.2 %constant_dynamic-slice_fusion.2 = (f32[4,1,16,1560]{3,2,1,0:T(8,128)S(1)}, f32[4,1,16,1560]{3,2,1,0:T(8,128)S(1)}) fusion(f32[4,2,16,1560]{3,2,1,0:T(8,128)} %bitcast.32, s32[]{:T(128)S(6)} %select_n.130, s32[]{:T(128)S(6)} %select_n.131), kind=kLoop, calls=%fused_computation.32 | loop fusion | bytes 1597448 | tf_op jit(solution)/shard_map/jit(dynamic_index_in_dim)/dynamic_slice | solution.py:366
  44.3 1.8 %collective-permute-start.5 = (f32[64,1560]{1,0:T(8,128)S(1)}, f32[64,1560]{1,0:T(8,128)S(1)}, u32[]{:S(2)}, u32[]{:S(2)}) collective-permute-start(f32[64,1560]{1,0:T(8,128)S(1)} %bitcast.38), channel_id=1, source_target_pairs={{0,1},{1,0},{2,3},{3,2},{4,5},{5,4},{6,7},{7,6},{8,9},{9,8},{10,11... | collective-permute-start | bytes 1198088 | tf_op jit(solution)/shard_map/ppermute | solution.py:336
  46.1 1.4 %collective-permute-done.6 = f32[8,1560]{1,0:T(8,128)S(1)} collective-permute-done((f32[8,1560]{1,0:T(8,128)}, f32[8,1560]{1,0:T(8,128)S(1)}, u32[]{:S(2)}, u32[]{:S(2)}) %collective-permute-start.6) | collective-permute-done | bytes 49952 | tf_op jit(solution)/shard_map/ppermute | solution.py:336
  47.5 0.8 add.115
  48.6 8.2 %collective-permute-done.7 = f32[8,1560]{1,0:T(8,128)S(1)} collective-permute-done((f32[8,1560]{1,0:T(8,128)S(1)}, f32[8,1560]{1,0:T(8,128)S(1)}, u32[]{:S(2)}, u32[]{:S(2)}) %collective-permute-start.7) | collective-permute-done | bytes 49952 | tf_op jit(solution)/shard_map/ppermute | solution.py:336
  57.0 1.9 %collective-permute-start.8 = (f32[40,1560]{1,0:T(8,128)S(1)}, f32[40,1560]{1,0:T(8,128)S(1)}, u32[]{:S(2)}, u32[]{:S(2)}) collective-permute-start(f32[40,1560]{1,0:T(8,128)S(1)} %pad_maximum_fusion.2), channel_id=1, source_target_pairs={{0,2},{1,3},{2,0},{3,1},{4,6},{5,7},{6,4},{7,5},{8,10},{9,11},{10,... | collective-permute-start | bytes 748808 | tf_op jit(solution)/shard_map/ppermute | solution.py:336
  58.9 5.3 %collective-permute-done.8 = f32[40,1560]{1,0:T(8,128)S(1)} collective-permute-done((f32[40,1560]{1,0:T(8,128)S(1)}, f32[40,1560]{1,0:T(8,128)S(1)}, u32[]{:S(2)}, u32[]{:S(2)}) %collective-permute-start.8) | collective-permute-done | bytes 249632 | tf_op jit(solution)/shard_map/ppermute | solution.py:336
  64.3 2.4 %collective-permute-start.9 = (f32[24,1560]{1,0:T(8,128)S(1)}, f32[24,1560]{1,0:T(8,128)S(1)}, u32[]{:S(2)}, u32[]{:S(2)}) collective-permute-start(f32[24,1560]{1,0:T(8,128)S(1)} %pad_maximum_fusion.3), channel_id=1, source_target_pairs={{0,4},{1,5},{2,6},{3,7},{4,0},{5,1},{6,2},{7,3},{8,12},{9,13},{10,... | collective-permute-start | bytes 449288 | tf_op jit(solution)/shard_map/ppermute | solution.py:336
  67.2 5.4 %collective-permute-done.9 = f32[24,1560]{1,0:T(8,128)S(1)} collective-permute-done((f32[24,1560]{1,0:T(8,128)S(1)}, f32[24,1560]{1,0:T(8,128)S(1)}, u32[]{:S(2)}, u32[]{:S(2)}) %collective-permute-start.9) | collective-permute-done | bytes 149792 | tf_op jit(solution)/shard_map/ppermute | solution.py:336
  73.3 4.6 %fit.1 = f32[16,24]{1,0:T(8,128)} custom-call(f32[16,1560]{1,0:T(8,128)} %slice_add_fusion.n_ref), custom_call_target="tpu_custom_call" | custom-call | tf_op jit(solution)/shard_map/fit/pallas_call | solution.py:382
  80.6 4.3 %model.1 = f32[64,512]{1,0:T(8,128)} custom-call(f32[8,1560]{1,0:T(8,128)} %slice_add_fusion.1.nb_ref, f32[10,24,512]{2,1,0:T(8,128)} %pad_maximum_fusion.1.t_ref, f32[10,24,128]{2,1,0:T(8,128)} %concatenate.26.x_ref, f32[10,24,512]{2,1,0:T(8,128)} %copy-done.4, f32[10,24,128]{2,1,0:T(8,128)} %copy-done.7, f32[14,64,512]{2,1,0:T(8,128)} %copy-done), custom_call_target="tpu_custom_call" | custom-call | tf_op jit(solution)/shard_map/model/pallas_call | solution.py:377
  84.9 5.9 %all-to-all-start = ((f32[8,8,512]{2,1,0:T(8,128)}), f32[8,8,512]{2,1,0:T(8,128)S(1)}, u32[]{:S(2)}, u32[]{:S(2)}) async-start(f32[8,8,512]{2,1,0:T(8,128)} %bitcast.35), calls=%async_computation | async-start | bytes 262144 | tf_op jit(solution)/shard_map/all_to_all | solution.py:381
  91.7 6.7 %all-to-all-done = f32[8,8,512]{2,1,0:T(8,128)S(1)} async-done(((f32[8,8,512]{2,1,0:T(8,128)}), f32[8,8,512]{2,1,0:T(8,128)S(1)}, u32[]{:S(2)}, u32[]{:S(2)}) %all-to-all-start) | async-done | bytes 131104 | tf_op jit(solution)/shard_map/all_to_all | solution.py:381
  98.4 0.8 subtract_multiply_fusion
  (60 shorter events, 7.9 us)
Async XLA Ops:
  2.1 2.4 %copy-start.2 = (f32[12,10,512]{2,0,1:T(8,128)S(1)}, f32[12,10,512]{2,0,1:T(8,128)}, u32[]{:S(2)}) copy-start(f32[12,10,512]{2,0,1:T(8,128)} %param.7) | copy-start | bytes 737284
  3.9 14.4 %copy-start = (f32[14,64,512]{2,1,0:T(8,128)}, f32[14,64,512]{2,1,0:T(8,128)S(1)}, u32[]{:S(2)}) copy-start(f32[14,64,512]{2,1,0:T(8,128)S(1)} %pad_maximum_fusion.own_ref.pack_ref) | copy-start | bytes 5505028
  3.9 14.4 %collective-permute-start.1 = (f32[14,64,512]{2,1,0:T(8,128)S(1)}, f32[14,64,512]{2,1,0:T(8,128)}, u32[]{:S(2)}, u32[]{:S(2)}) collective-permute-start(f32[14,64,512]{2,1,0:T(8,128)S(1)} %pad_maximum_fusion.own_ref.pack_ref), channel_id=1, source_target_pairs={{0,8},{8,0},{16,24},{24,16},{1,9},{9,1},{17,25},{25,17},{2,10},{10... | collective-permute-start | bytes 5505032 | tf_op jit(solution)/shard_map/ppermute | solution.py:336
  4.6 5.9 %collective-permute-start.2 = (f32[10,12,10]{2,1,0:T(8,128)S(1)}, f32[10,12,10]{2,1,0:T(8,128)S(1)}, u32[]{:S(2)}, u32[]{:S(2)}) collective-permute-start(f32[10,12,10]{2,1,0:T(8,128)S(1)} %pad_maximum_fusion.5), channel_id=1, source_target_pairs={{0,16},{8,24},{16,0},{24,8},{1,17},{9,25},{17,1},{25,9},{2,18},{10... | collective-permute-start | bytes 14408 | tf_op jit(solution)/shard_map/ppermute | solution.py:336
  7.2 10.1 %collective-permute-start = (f32[10,12,512]{2,1,0:T(8,128)S(1)}, f32[10,12,512]{2,1,0:T(8,128)S(1)}, u32[]{:S(2)}, u32[]{:S(2)}) collective-permute-start(f32[10,12,512]{2,1,0:T(8,128)S(1)} %bitcast.27), channel_id=1, source_target_pairs={{0,16},{8,24},{16,0},{24,8},{1,17},{9,25},{17,1},{25,9},{2,18},{10... | collective-permute-start | bytes 737288 | tf_op jit(solution)/shard_map/ppermute | solution.py:336
  10.7 28.2 %collective-permute-start.3 = (f32[10,24,5]{2,1,0:T(8,128)S(1)}, f32[10,24,5]{2,1,0:T(8,128)S(1)}, u32[]{:S(2)}, u32[]{:S(2)}) collective-permute-start(f32[10,24,5]{2,1,0:T(8,128)S(1)} %get-tuple-element.27), channel_id=1, source_target_pairs={{0,1},{1,2},{2,3},{3,4},{4,5},{5,6},{6,7},{8,9},{9,10},{10,11},{11... | collective-permute-start | bytes 14408 | tf_op jit(solution)/shard_map/ppermute | solution.py:351
  14.6 24.3 %collective-permute-start.4 = (f32[10,24,5]{2,1,0:T(8,128)S(1)}, f32[10,24,5]{2,1,0:T(8,128)S(1)}, u32[]{:S(2)}, u32[]{:S(2)}) collective-permute-start(f32[10,24,5]{2,1,0:T(8,128)S(1)} %get-tuple-element.26), channel_id=1, source_target_pairs={{1,0},{2,1},{3,2},{4,3},{5,4},{6,5},{7,6},{9,8},{10,9},{11,10},{12... | collective-permute-start | bytes 14408 | tf_op jit(solution)/shard_map/ppermute | solution.py:352
  44.3 12.6 %collective-permute-start.5 = (f32[64,1560]{1,0:T(8,128)S(1)}, f32[64,1560]{1,0:T(8,128)S(1)}, u32[]{:S(2)}, u32[]{:S(2)}) collective-permute-start(f32[64,1560]{1,0:T(8,128)S(1)} %bitcast.38), channel_id=1, source_target_pairs={{0,1},{1,0},{2,3},{3,2},{4,5},{5,4},{6,7},{7,6},{8,9},{9,8},{10,11... | collective-permute-start | bytes 1198088 | tf_op jit(solution)/shard_map/ppermute | solution.py:336
  46.0 1.4 %collective-permute-start.6 = (f32[8,1560]{1,0:T(8,128)}, f32[8,1560]{1,0:T(8,128)S(1)}, u32[]{:S(2)}, u32[]{:S(2)}) collective-permute-start(f32[8,1560]{1,0:T(8,128)} %get-tuple-element.17), channel_id=1, source_target_pairs={{0,8},{8,0},{16,24},{24,16},{1,9},{9,1},{17,25},{25,17},{2,10},{10... | collective-permute-start | bytes 149768 | tf_op jit(solution)/shard_map/ppermute | solution.py:336
  48.3 8.5 %collective-permute-start.7 = (f32[8,1560]{1,0:T(8,128)S(1)}, f32[8,1560]{1,0:T(8,128)S(1)}, u32[]{:S(2)}, u32[]{:S(2)}) collective-permute-start(f32[8,1560]{1,0:T(8,128)S(1)} %add.115), channel_id=1, source_target_pairs={{0,1},{1,0},{2,3},{3,2},{4,5},{5,4},{6,7},{7,6},{8,9},{9,8},{10,11... | collective-permute-start | bytes 149768 | tf_op jit(solution)/shard_map/ppermute | solution.py:336
  56.9 9.8 %copy-start.1 = (f32[10,24,512]{2,1,0:T(8,128)S(1)}, f32[10,24,512]{2,1,0:T(8,128)}, u32[]{:S(2)}) copy-start(f32[10,24,512]{2,1,0:T(8,128)} %pad_maximum_fusion.1.t_ref) | copy-start | bytes 1474564
  56.9 9.8 %copy-start.3 = (f32[10,24,128]{2,1,0:T(8,128)S(1)}, f32[10,24,128]{2,1,0:T(8,128)}, u32[]{:S(2)}) copy-start(f32[10,24,128]{2,1,0:T(8,128)} %concatenate.26.x_ref) | copy-start | bytes 368644
  57.0 7.2 %collective-permute-start.8 = (f32[40,1560]{1,0:T(8,128)S(1)}, f32[40,1560]{1,0:T(8,128)S(1)}, u32[]{:S(2)}, u32[]{:S(2)}) collective-permute-start(f32[40,1560]{1,0:T(8,128)S(1)} %pad_maximum_fusion.2), channel_id=1, source_target_pairs={{0,2},{1,3},{2,0},{3,1},{4,6},{5,7},{6,4},{7,5},{8,10},{9,11},{10,... | collective-permute-start | bytes 748808 | tf_op jit(solution)/shard_map/ppermute | solution.py:336
  64.3 8.3 %collective-permute-start.9 = (f32[24,1560]{1,0:T(8,128)S(1)}, f32[24,1560]{1,0:T(8,128)S(1)}, u32[]{:S(2)}, u32[]{:S(2)}) collective-permute-start(f32[24,1560]{1,0:T(8,128)S(1)} %pad_maximum_fusion.3), channel_id=1, source_target_pairs={{0,4},{1,5},{2,6},{3,7},{4,0},{5,1},{6,2},{7,3},{8,12},{9,13},{10,... | collective-permute-start | bytes 449288 | tf_op jit(solution)/shard_map/ppermute | solution.py:336
  66.7 12.5 %collective-permute-start.11 = (f32[10,24,512]{2,1,0:T(8,128)S(1)}, f32[10,24,512]{2,1,0:T(8,128)S(1)}, u32[]{:S(2)}, u32[]{:S(2)}) collective-permute-start(f32[10,24,512]{2,1,0:T(8,128)S(1)} %copy-done.1), channel_id=1, source_target_pairs={{0,8},{8,0},{16,24},{24,16},{1,9},{9,1},{17,25},{25,17},{2,10},{10... | collective-permute-start | bytes 1474568 | tf_op jit(solution)/shard_map/ppermute | solution.py:336
  66.7 12.5 %collective-permute-start.12 = (f32[10,24,128]{2,1,0:T(8,128)S(1)}, f32[10,24,128]{2,1,0:T(8,128)S(1)}, u32[]{:S(2)}, u32[]{:S(2)}) collective-permute-start(f32[10,24,128]{2,1,0:T(8,128)S(1)} %copy-done.3), channel_id=1, source_target_pairs={{0,8},{8,0},{16,24},{24,16},{1,9},{9,1},{17,25},{25,17},{2,10},{10... | collective-permute-start | bytes 368648 | tf_op jit(solution)/shard_map/ppermute | solution.py:336
  78.5 12.3 %collective-permute-start.10 = (f32[8,24]{1,0:T(8,128)S(1)}, f32[8,24]{1,0:T(8,128)S(1)}, u32[]{:S(2)}, u32[]{:S(2)}) collective-permute-start(f32[8,24]{1,0:T(8,128)S(1)} %get-tuple-element.29), channel_id=1, source_target_pairs={{0,8},{8,0},{16,24},{24,16},{1,9},{9,1},{17,25},{25,17},{2,10},{10... | collective-permute-start | bytes 2312 | tf_op jit(solution)/shard_map/ppermute | solution.py:336
  79.2 19.3 %copy-start.5 = (f32[8,3,4096]{2,0,1:T(8,128)S(1)}, f32[8,3,4096]{2,0,1:T(8,128)}, u32[]{:S(2)}) copy-start(f32[8,3,4096]{2,0,1:T(8,128)} %param.12) | copy-start | bytes 1179652
  79.2 19.3 %copy-start.6 = (s32[8,3,4096]{2,0,1:T(8,128)S(1)}, s32[8,3,4096]{2,0,1:T(8,128)}, u32[]{:S(2)}) copy-start(s32[8,3,4096]{2,0,1:T(8,128)} %param.13) | copy-start | bytes 1179652
  79.2 0.8 copy-start.4
  80.0 0.6 copy-start.7
  84.9 13.5 %all-to-all-start = ((f32[8,8,512]{2,1,0:T(8,128)}), f32[8,8,512]{2,1,0:T(8,128)S(1)}, u32[]{:S(2)}, u32[]{:S(2)}) async-start(f32[8,8,512]{2,1,0:T(8,128)} %bitcast.35), calls=%async_computation | async-start | bytes 262144 | tf_op jit(solution)/shard_map/all_to_all | solution.py:381

commit v3 on v2

v3 whole, which is shorter than its diff:
```python
import jax
import jax.numpy as jnp
from jax import lax
from jax.experimental import pallas as pl
from jax.experimental.pallas import tpu as pltpu
from jax.sharding import PartitionSpec as P


LANES = 128
BF = jnp.bfloat16


def split(x):
    hi = x.astype(BF)
    return hi, (x - hi.astype(jnp.float32)).astype(BF)


def dot(x, w):
    return jnp.dot(x, w, preferred_element_type=jnp.float32)


def pair_list(K):
    return [(k, l) for k in range(K) for l in range(k, K)]


def put(h_ref, row, lane, width, v):
    hi, lo = split(v)
    h_ref[row:row + 8, lane:lane + v.shape[1]] = hi
    h_ref[row:row + 8, width + lane:width + lane + v.shape[1]] = lo


def pair_block(h_ref, t, s, row, Z, lane, width):
    for i, (k, l) in enumerate(pair_list(len(t))):
        put(h_ref, i * Z + row, lane, width, t[k] * s[l] + t[l] * s[k])


def single_block(h_ref, t, row, Z, lane, width):
    for k in range(len(t)):
        put(h_ref, k * Z + row, lane, width, t[k])


def split_dot(h, w):
    return dot(h, jnp.concatenate([w, w], axis=0))


def place_of(best, me, zo, ns, Z):
    best = best.astype(jnp.int32)
    block = jnp.zeros_like(best)
    for j in range(1, ns):
        block = block + jnp.where(best >= j * zo, 1, 0)
    rel = block ^ me
    return (rel & 1) * Z + (rel >> 1) * zo + best - block * zo


def make_main(K, Z, band, S, W):
    pairs = pair_list(K)
    NP = len(pairs)
    ZB = Z // 8
    half = band // 2
    wide = W + LANES
    top = 24
    N = 2 * S
    step = 16

    def band_matrix(own_ref, other_ref, wb_ref, a_ref, rhs_ref, edge_ref, aeb_ref):
        root_own = jnp.sqrt(own_ref[band])
        root_other = jnp.sqrt(other_ref[band])
        zero = jnp.zeros((band + 1, top, N), jnp.float32)
        wb_ref[:, :top, :] = zero
        wb_ref[:, top + W:, :] = zero
        for d in range(band + 1):
            src = d if d < band else band + 1
            both = jnp.concatenate([own_ref[src] * root_own, other_ref[src] * root_other], axis=0)
            wb_ref[d, top:top + W, :] = both.T

        def block(i, _):
            base = pl.multiple_of(i * step, step)
            for part in range(step // 8):
                acc = [None] * (band + 1)
                for d in range(band):
                    rows = pl.ds(base + (part * 8 + top - step + half - d), 8)
                    v = [wb_ref[e, rows, :] for e in range(d, band + 1)]
                    for e in range(d, band + 1):
                        o = e - d if e < band else band
                        p = v[0] * v[e - d]
                        acc[o] = p if acc[o] is None else acc[o] + p
                acc[0] = acc[0] * 0.5
                for o in range(band + 1):
                    a_ref[o, pl.ds(base + part * 8, 8), :] = acc[o]
            for o in range(band + 1):
                hi, lo = split(a_ref[o, pl.ds(base, step), :])
                rhs_ref[o, pl.ds(base, step), :N] = hi
                rhs_ref[o, pl.ds(base, step), N:] = lo
            return 0

        lax.fori_loop(0, (W + 2 * step) // step, block, 0)
        edge_ref[...] = jnp.zeros_like(edge_ref)
        for o in range(band):
            edge_ref[0, 2 * half * o:2 * half * o + half, :] = a_ref[o, step - half:step, :]
            edge_ref[0, 2 * half * o + half:2 * half * (o + 1), :] = a_ref[o, step + W - o:step + W - o + half, :]
        edge_ref[1, :half, :] = a_ref[band, step - half:step, :]
        edge_ref[1, half:2 * half, :] = a_ref[band, step + W:step + W + half, :]
        for o in range(2):
            hi, lo = split(edge_ref[o])
            aeb_ref[o, :, :N] = hi
            aeb_ref[o, :, N:] = lo

    def kernel(t_ref, own_ref, other_ref, out_ref, aeb_ref,
               wb_ref, a_ref, rhs_ref, edge_ref, s_ref, h0_ref, h1_ref, acc_ref):
        band_matrix(own_ref, other_ref, wb_ref, a_ref, rhs_ref, edge_ref, aeb_ref)
        s_ref[:, :, :W] = t_ref[...]
        s_ref[:, :, W:] = jnp.zeros((K, Z, LANES), jnp.float32)
        acc_ref[...] = jnp.zeros_like(acc_ref)

        G = 2 * LANES

        def build(h_ref):
            for b in range(ZB):
                rows = pl.ds(b * 8, 8)
                for q in range(W // G):
                    t = [t_ref[k, rows, pl.ds(q * G, G)] for k in range(K)]
                    s = [s_ref[k, rows, pl.ds(q * G, G)] for k in range(K)]
                    pair_block(h_ref, t, s, b * 8, Z, q * G, W)

        def advance():
            for k in range(K):
                for b in range(ZB):
                    rows = pl.ds(b * 8, 8)
                    s_ref[k, rows, :] = pltpu.roll(s_ref[k, rows, :], wide - 1, 1)

        def add(h_ref, first, count, w):
            acc_ref[first:first + count] += split_dot(h_ref[:count], w)

        def weights(o):
            return rhs_ref[o, step:step + W, :]

        build(h0_ref)
        advance()

        def pair_step(i, _):
            build(h1_ref)
            advance()
            add(h0_ref, 0, NP * Z, weights(2 * i))
            build(h0_ref)
            advance()
            add(h1_ref, 0, NP * Z, weights(2 * i + 1))
            return 0

        lax.fori_loop(0, band // 2, pair_step, 0)
        for b in range(ZB):
            for q in range(W // G):
                single_block(h1_ref, [t_ref[k, pl.ds(b * 8, 8), pl.ds(q * G, G)] for k in range(K)], b * 8, Z, q * G, W)
        add(h0_ref, 0, NP * Z, weights(band - 1))
        add(h1_ref, NP * Z, K * Z, weights(band))
        out_ref[...] = acc_ref[:, :N] + acc_ref[:, N:]

    return pl.pallas_call(
        kernel,
        out_shape=(jax.ShapeDtypeStruct(((NP + K) * Z, N), jnp.float32),
                   jax.ShapeDtypeStruct((2, LANES, 2 * N), BF)),
        scratch_shapes=[pltpu.VMEM((band + 1, W + 2 * top, N), jnp.float32),
                        pltpu.VMEM((band + 1, W + 2 * step, N), jnp.float32),
                        pltpu.VMEM((band + 1, W + 2 * step, 2 * N), BF),
                        pltpu.VMEM((2, LANES, N), jnp.float32),
                        pltpu.VMEM((K, Z, wide), jnp.float32),
                        pltpu.VMEM((NP * Z, 2 * W), BF),
                        pltpu.VMEM((NP * Z, 2 * W), BF),
                        pltpu.VMEM(((NP + K) * Z, 2 * N), jnp.float32)],
        compiler_params=pltpu.CompilerParams(vmem_limit_bytes=60 << 20),
        name="normals")


def make_edge(K, Z, band, S, own, ns):
    NP = K * (K + 1) // 2
    ZB = Z // 8
    half = band // 2
    N = 2 * S

    def kernel(acc_ref, aeb_ref, x_ref, own_ref, other_ref, me_ref, left_ref, right_ref, nb_ref, nb2_ref, h_ref):
        inp = lax.broadcasted_iota(jnp.int32, (LANES, LANES), 0)
        outp = lax.broadcasted_iota(jnp.int32, (LANES, LANES), 1)
        dd = outp // (2 * half)
        ii = outp % (2 * half)
        isl = ii < half
        valid = outp < 2 * half * band
        src1 = jnp.where(isl, ii, 64 + half + ii)
        src2 = jnp.where(isl, ii + dd, 64 + half + ii - dd)
        sel1 = ((inp == src1) & valid).astype(jnp.float32).astype(BF)
        sel2 = ((inp == src2) & valid).astype(jnp.float32).astype(BF)
        x = x_ref[...].reshape(K * Z, LANES)
        hi = x.astype(BF)
        rest = x - hi.astype(jnp.float32)
        mid, low = split(rest)
        picks = jnp.concatenate([sel1, sel2], axis=1)
        e = (dot(hi, picks) + dot(mid, picks)) + dot(low, picks)
        e1 = e[:, :LANES].reshape(K, Z, LANES)
        e2 = e[:, LANES:].reshape(K, Z, LANES)
        for b in range(ZB):
            t = [e1[k, b * 8:(b + 1) * 8] for k in range(K)]
            s = [e2[k, b * 8:(b + 1) * 8] for k in range(K)]
            pair_block(h_ref, t, s, b * 8, Z, 0, LANES)
            single_block(h_ref.at[NP * Z:], t, b * 8, Z, 0, LANES)
        sums = []
        for part, o in ((h_ref[:NP * Z], 0), (h_ref[NP * Z:], 1)):
            v = split_dot(part, aeb_ref[o])
            sums.append(v[:, :N] + v[:, N:])
        acc = acc_ref[...] + jnp.concatenate(sums, axis=0)
        best = jnp.concatenate([own_ref[...], other_ref[...]], axis=1)
        hit = lax.broadcasted_iota(jnp.int32, (Z, N), 0) == place_of(best, me_ref[...], Z * 2 // ns, ns, Z)
        nb_ref[...] = jnp.zeros_like(nb_ref)
        nb2_ref[...] = jnp.zeros_like(nb2_ref)
        for n in range(NP + K):
            item = acc[n * Z:(n + 1) * Z]
            best = jnp.sum(jnp.where(hit, item, 0.0), axis=0, keepdims=True)
            row, at = n % R, (n // R) * LANES
            nb_ref[row:row + 1, at:at + S] = best[:, :S]
            nb2_ref[row:row + 1, at:at + S] = best[:, S:]
        full = acc.T
        for w in range(S // own):
            block = jnp.concatenate([full[own * w:own * (w + 1)], full[S + own * w:S + own * (w + 1)]], axis=0)
            left_ref[R * w:R * (w + 1)] = block[:, :cut]
            right_ref[R * w:R * (w + 1)] = block[:, cut:]

    n = (NP + K) * Z
    R = 2 * own
    cut = -(-n // (2 * LANES)) * LANES
    width = -(-(NP + K) // R) * LANES

    def whole(*shape):
        return pl.BlockSpec(shape, lambda i: (0,) * len(shape))

    rows = (NP + K) * Z
    return pl.pallas_call(
        kernel, grid=(1,),
        out_shape=tuple(jax.ShapeDtypeStruct(shape, jnp.float32) for shape in ((N, cut), (N, n - cut), (R, width), (R, width))),
        out_specs=(whole(N, cut), whole(N, n - cut), whole(R, width), whole(R, width)),
        in_specs=[whole(rows, N), whole(2, LANES, 2 * N), whole(K, Z, LANES),
                  whole(1, S), whole(1, S), whole(1, 1)],
        scratch_shapes=[pltpu.VMEM(((NP + K) * Z, 2 * LANES), BF)],
        compiler_params=pltpu.CompilerParams(vmem_limit_bytes=60 << 20),
        name="edges")


def factor_solve(N, proj):
    K = len(proj)
    L, inv, y = {}, [], []
    for j in range(K):
        for i in range(j, K):
            v = N[(j, i)]
            for m in range(j):
                v = v - L[(i, m)] * L[(j, m)]
            L[(i, j)] = v
        inv.append(1.0 / jnp.sqrt(L[(j, j)]))
        for i in range(j + 1, K):
            L[(i, j)] = L[(i, j)] * inv[j]
        v = proj[j]
        for m in range(j):
            v = v - L[(j, m)] * y[m]
        y.append(v * inv[j])
    c = [None] * K
    for j in reversed(range(K)):
        v = y[j]
        for i in range(j + 1, K):
            v = v - L[(i, j)] * c[i]
        c[j] = v * inv[j]
    return c


def fit_kernel_for(K, Z):
    pairs = pair_list(K)
    NP = len(pairs)

    def kernel(n_ref, gain_ref):
        n = n_ref[...].T
        proj = [n[(NP + k) * Z:(NP + k + 1) * Z] for k in range(K)]
        c = factor_solve({kl: n[i * Z:(i + 1) * Z] for i, kl in enumerate(pairs)}, proj)
        chi = proj[0] * c[0]
        for k in range(1, K):
            chi = chi + proj[k] * c[k]
        gain_ref[...] = jnp.log1p(chi / K).T

    return kernel


def model_kernel_for(K, Z, band, ns):
    pairs = pair_list(K)
    NP = len(pairs)
    half = band // 2
    hp = lax.Precision.HIGHEST

    def kernel(nb_ref, t_ref, x_ref, t2_ref, x2_ref, pack_ref, best_ref, me_ref, model_ref):
        S, W = model_ref.shape

        def best(n):
            rows = nb_ref.shape[0]
            at = (n // rows) * LANES
            return nb_ref[n % rows:n % rows + 1, at:at + S]

        c = factor_solve({kl: best(i) for i, kl in enumerate(pairs)}, [best(NP + k) for k in range(K)])
        pad = jnp.zeros((LANES - K, S), jnp.float32)
        coef = jnp.concatenate(c + [pad], axis=0).T
        place = place_of(jnp.broadcast_to(best_ref[...].astype(jnp.float32), (S, S)).T[:, :1], me_ref[...], Z * 2 // ns, ns, Z)
        lane = lax.broadcasted_iota(jnp.int32, (S, K * Z), 1)
        cols = jnp.zeros((S, K * Z), jnp.float32)
        for k in range(K):
            cols = jnp.where(lane // Z == k, coef[:, k:k + 1], cols)
        main, edge = None, None
        for part, (a_ref, b_ref) in enumerate(((t_ref, x_ref), (t2_ref, x2_ref))):
            sel = jnp.where(lane % Z + part * Z == place, cols, 0.0)
            m = jnp.dot(sel, a_ref[...].reshape(K * Z, W), precision=hp, preferred_element_type=jnp.float32)
            e = jnp.dot(sel, b_ref[...].reshape(K * Z, LANES), precision=hp, preferred_element_type=jnp.float32)
            main = m if main is None else main + m
            edge = e if edge is None else edge + e
        lane = lax.broadcasted_iota(jnp.int32, (S, LANES), 1)
        right = pltpu.roll(edge, LANES - (64 + 2 * half), 1)
        left = pltpu.roll(edge, LANES - half, 1)
        last = jnp.where(lane < half, right, jnp.where(lane >= LANES - half, left, 0.0))
        u = jnp.concatenate([main, last], axis=1)
        wide = W + LANES
        total = None
        for d in range(band):
            shift = (half - d) % wide
            v = (pltpu.roll(u, shift, 1) if shift else u)[:, :W]
            term = pack_ref[d] * v
            total = term if total is None else total + term
        model_ref[...] = total

    return kernel


def body(templates, resolution, coadd_flux, coadd_ivar, best_index, exposures, exposure_mask):
    S, band, W = resolution.shape
    half = band // 2
    zo, K, _ = templates.shape
    nw, ns = lax.axis_size("wave"), lax.axis_size("spec")
    Z = zo * ns // 2
    own = S // nw
    me, wave = lax.axis_index("spec"), lax.axis_index("wave")

    def swap(x, axis, m):
        return lax.ppermute(x, axis, [(i, i ^ m) for i in range(lax.axis_size(axis))])

    ys = range(2, ns, 2)
    block = jnp.transpose(templates, (1, 0, 2))
    flat = block.reshape(K * zo, W)
    others = [swap(flat, "spec", m).reshape(K, zo, W) for m in ys]
    ends = jnp.concatenate([templates[:, :, W - half:], templates[:, :, :half]], axis=2)
    ends = jnp.transpose(ends, (2, 0, 1)).reshape(2 * half, zo * K)
    ends = jnp.concatenate([ends] + [swap(ends, "spec", m) for m in ys], axis=1)
    before = lax.ppermute(ends[:half], "wave", [(i, i + 1) for i in range(nw - 1)])
    after = lax.ppermute(ends[half:], "wave", [(i + 1, i) for i in range(nw - 1)])
    pack = jnp.concatenate([jnp.transpose(resolution, (1, 0, 2)), coadd_ivar[None], coadd_flux[None]], axis=0)
    other_pack = swap(pack, "spec", 1)
    wanted = best_index.reshape(1, S)
    other_wanted = swap(wanted, "spec", 1)
    t = jnp.concatenate([block] + others, axis=1)
    index = jnp.full((1, 1), me, jnp.int32)
    acc, aeb = make_main(K, Z, band, S, W)(t, pack, other_pack)
    acc, before, after = lax.optimization_barrier((acc, before, after))
    gap = jnp.zeros((K, Z, 64 - 3 * half), jnp.float32)
    before, after = (jnp.transpose(v.reshape(half, Z, K), (2, 1, 0)) for v in (before, after))
    x = jnp.concatenate([before, t[:, :, :2 * half], gap, t[:, :, W - 2 * half:], after, gap], axis=2)
    t2, x2 = swap(t, "spec", 1), swap(x, "spec", 1)
    left, right, nb, nb2 = make_edge(K, Z, band, S, own, ns)(acc, aeb, x, wanted, other_wanted, index)

    R = 2 * own

    def halve(d, bit, order, extra=None):
        axis = order.index(bit)
        b = (wave // bit) % 2
        columns = d.shape[-1]
        keep = lax.dynamic_index_in_dim(d, b, axis, keepdims=False)
        send = lax.dynamic_index_in_dim(d, 1 - b, axis, keepdims=False).reshape(-1, columns)
        rows = send.shape[0]
        if extra is not None:
            send = jnp.concatenate([send, jnp.tile(extra, (rows // R, 1))], axis=1)
        got = swap(send, "wave", bit)
        if extra is not None:
            extra = extra + got[:R, columns:]
        d = keep + got[:rows, :columns].reshape(keep.shape)
        return d, order[:axis] + order[axis + 1:], extra

    bits = [1 << i for i in range(nw.bit_length() - 1)]
    order = bits[::-1]
    left, right = (v.reshape([2] * len(bits) + [R, v.shape[1]]) for v in (left, right))
    left, order_a, _ = halve(left, bits[0], order)
    right, order_b, _ = halve(right, bits[1], order)
    nb = nb + swap(nb2, "spec", 1)
    got = swap(nb, "wave", bits[0])
    left, order_a, _ = halve(left, bits[1], order_a)
    right, order_b, _ = halve(right, bits[0], order_b)
    nb = nb + got
    nb = nb + swap(nb, "wave", bits[1])
    d = jnp.concatenate([left, right], axis=-1)
    for bit in bits[2:]:
        d, order_a, nb = halve(d, bit, order_a, nb)
    model = pl.pallas_call(
        model_kernel_for(K, Z, band, ns), out_shape=jax.ShapeDtypeStruct((S, W), jnp.float32),
        compiler_params=pltpu.CompilerParams(vmem_limit_bytes=60 << 20), name="model",
    )(nb, t, x, t2, x2, pack, wanted, index)
    rows = lax.all_to_all(model.reshape(nw, own, W), "wave", 0, 0, tiled=True)
    gain = pl.pallas_call(
        fit_kernel_for(K, Z), out_shape=jax.ShapeDtypeStruct((2 * own, Z), jnp.float32), name="fit",
    )(d)
    halves = jnp.stack([gain[:own], swap(gain[own:], "spec", 1)], axis=0).reshape(2, own, ns // 2, zo)
    gain = jnp.transpose(halves, (1, 2, 0, 3)).reshape(own, ns, zo)
    bit = 1
    while bit < ns:
        flipped = gain.reshape(own, ns // (2 * bit), 2, bit, zo)[:, :, ::-1].reshape(own, ns, zo)
        gain = jnp.where((me // bit) % 2 == 1, flipped, gain)
        bit *= 2
    gain = gain.reshape(own, ns * zo)
    rows = jnp.transpose(rows, (1, 0, 2)).reshape(own, 1, nw * W)
    residuals = exposure_mask.astype(jnp.float32) * (exposures - rows)
    return gain, residuals


def solution(mesh):
    in_specs = (
        P("spec", None, "wave"),
        P("spec", None, "wave"),
        P("spec", "wave"),
        P("spec", "wave"),
        P("spec"),
        P(("spec", "wave"), None, None),
        P(("spec", "wave"), None, None),
    )
    out_specs = (P(("spec", "wave"), None), P(("spec", "wave"), None, None))

    return jax.shard_map(body, mesh=mesh, in_specs=in_specs, out_specs=out_specs, check_vma=False)
```

time: 99.7 us -> 97.3 us (0.976)
  Pallas kernels: 32.7 us -> 28 us
  starting transfers between devices: 21.2 us -> 24.7 us
  waiting for transfers between devices: 31.7 us -> 28.7 us
  local copies, waits for them, and re-layouts: 5.33 us -> 7.6 us
    ppermute x11 -> x15, starting transfers between devices: 10.1 us -> 15.7 us  [swap(): lax.ppermute(x, axis, [(i, i ^ m) for i in range(lax.axis_size(axis))])]
    ppermute x11 -> x15, waiting for transfers between devices: 25 us -> 21.9 us  [swap(): lax.ppermute(x, axis, [(i, i ^ m) for i in range(lax.axis_size(axis))])]
    pallas_call x1, Pallas kernels: 4.57 us -> 2 us  [body(): pl.pallas_call(fit_kernel_for(K, Z), out_shape=jax.ShapeDtypeStruct((2 *...]
    all_to_all x1, starting transfers between devices: 5.88 us -> 4.07 us  [body(): rows = lax.all_to_all(model.reshape(nw, own, W), 'wave', 0, 0, tiled=True)]
    pallas_call x1, Pallas kernels: 20.6 us -> 18.9 us  [body(): acc, aeb = make_main(K, Z, band, S, W)(t, pack, other_pack)]
    convert_element_type x2 -> x0, other arithmetic: 1.36 us -> none  [place_for(): return (rel % 2 * Z + rel // 2 * zo + best_index % zo).astype(jnp.float32)]
    add x6 -> x8, other arithmetic: 1.38 us -> 2.39 us  [the longest x5 1.67 us: halve(): d = keep + got[:rows, :columns].reshape(keep.shape)]
    dynamic_slice x2 -> x4, local copies, waits for them, and re-layouts: 1.22 us -> 2.05 us  [halve(): lax.dynamic_index_in_dim(d, 1 - b, axis, keepdims=False)]
  transfers between devices with their start and end apart: 14 -> 18, of which waited for: 7 -> 7; matrix products, arithmetic and copies ran while one was open for 5% -> 10% of each run, Pallas kernels for 30% -> 26%
where the time goes in v3:
time: 97.3 us; the launch traced here: 96.8 us
  waiting for transfers between devices  28.7 us (29%)
  Pallas kernels  28 us (29%)
  starting transfers between devices  24.7 us (25%)
  local copies, waits for them, and re-layouts  7.6 us (8%)
  other arithmetic  7.01 us (7%)
    ppermute x15, waiting for transfers between devices, swap(): lax.ppermute(x, axis, [(i, i ^ m) for i in range(lax.axis_size(axis))])  21.9 us
    pallas_call x1, Pallas kernels, body(): acc, aeb = make_main(K, Z, band, S, W)(t, pack, other_pack)  18.9 us
    ppermute x15, starting transfers between devices, swap(): lax.ppermute(x, axis, [(i, i ^ m) for i in range(lax.axis_size(axis))])  15.7 us
    all_to_all x1, waiting for transfers between devices, body(): rows = lax.all_to_all(model.reshape(nw, own, W), 'wave', 0, 0, tiled=True)  6.78 us
    pallas_call x1, Pallas kernels, body(): pl.pallas_call(model_kernel_for(K, Z, band, ns), out_shape=jax.ShapeDtype...  4.14 us
    all_to_all x1, starting transfers between devices, body(): rows = lax.all_to_all(model.reshape(nw, own, W), 'wave', 0, 0, tiled=True)  4.07 us
    ppermute x1, starting transfers between devices, body(): lax.ppermute(ends[:half], 'wave', [(i, i + 1) for i in range(nw - 1)])  3.61 us
    pallas_call x1, Pallas kernels, body(): make_edge(K, Z, band, S, own, ns)(acc, aeb, x, wanted, other_wanted, index)  2.97 us
  transfers between devices with their start and end apart: 18, of which 7 were waited for; matrix products, arithmetic and copies ran while one was open for 10% of the time, Pallas kernels for 26%

profile of v3, /device:TPU:0, one launch (start us, length us, event | category | flops | bytes accessed | tf_op | source)
XLA Modules:
  0.0 96.8 jit_solution(7102613174433815469)
XLA Ops:
  0.7 1.8 %pad_maximum_fusion.own_ref.pack_ref = f32[13,64,512]{2,1,0:T(8,128)S(1)} fusion(f32[1,64,512]{2,1,0:T(8,128)} %bitcast.60, f32[1,64,512]{2,1,0:T(8,128)} %bitcast.61, f32[11,64,512]{2,1,0:T(8,128)} %bitcast.47), kind=kLoop, calls=%fused_computation | loop fusion | flops 851968 | bytes 3407872 | tf_op jit(solution)/shard_map/concatenate | solution.py:352
  3.0 2.6 %collective-permute-start = (f32[120,512]{1,0:T(8,128)S(1)}, f32[120,512]{1,0:T(8,128)S(1)}, u32[]{:S(2)}, u32[]{:S(2)}) collective-permute-start(f32[120,512]{1,0:T(8,128)S(1)} %reshape.87), channel_id=1, source_target_pairs={{0,16},{8,24},{16,0},{24,8},{1,17},{9,25},{17,1},{25,9},{2,18},{10... | collective-permute-start | bytes 737288 | tf_op jit(solution)/shard_map/ppermute | solution.py:341
  6.5 5.9 %collective-permute-done.2 = f32[10,120]{1,0:T(8,128)S(1)} collective-permute-done((f32[10,120]{1,0:T(8,128)S(1)}, f32[10,120]{1,0:T(8,128)S(1)}, u32[]{:S(2)}, u32[]{:S(2)}) %collective-permute-start.2) | collective-permute-done | bytes 4832 | tf_op jit(solution)/shard_map/ppermute | solution.py:341
  12.5 3.6 %collective-permute-start.3 = (f32[5,240]{1,0:T(8,128)S(1)}, f32[5,240]{1,0:T(8,128)S(1)}, u32[]{:S(2)}, u32[]{:S(2)}) collective-permute-start(f32[5,240]{1,0:T(8,128)S(1)} %get-tuple-element.25), channel_id=1, source_target_pairs={{0,1},{1,2},{2,3},{3,4},{4,5},{5,6},{6,7},{8,9},{9,10},{10,11},{11... | collective-permute-start | bytes 14408 | tf_op jit(solution)/shard_map/ppermute | solution.py:350
  16.1 1.3 %collective-permute-start.4 = (f32[5,240]{1,0:T(8,128)S(1)}, f32[5,240]{1,0:T(8,128)S(1)}, u32[]{:S(2)}, u32[]{:S(2)}) collective-permute-start(f32[5,240]{1,0:T(8,128)S(1)} %get-tuple-element.24), channel_id=1, source_target_pairs={{1,0},{2,1},{3,2},{4,3},{5,4},{6,5},{7,6},{9,8},{10,9},{11,10},{12... | collective-permute-start | bytes 14408 | tf_op jit(solution)/shard_map/ppermute | solution.py:351
  17.4 0.9 pad_maximum_fusion.1.t_ref
  18.4 18.9 %normals.1 = (f32[1560,128]{1,0:T(8,128)}, bf16[2,128,256]{2,1,0:T(8,128)(2,1)}) custom-call(f32[10,24,512]{2,1,0:T(8,128)} %pad_maximum_fusion.1.t_ref, f32[13,64,512]{2,1,0:T(8,128)} %copy-done, f32[13,64,512]{2,1,0:T(8,128)} %collective-permute-done.1.other_ref), custom_call_target="tpu_custom_call" | custom-call | tf_op jit(solution)/shard_map/normals/pallas_call | solution.py:358
  38.0 0.9 concatenate.26.x_ref
  39.4 3.0 %edges.1 = (f32[128,896]{1,0:T(8,128)}, f32[128,664]{1,0:T(8,128)}, f32[16,640]{1,0:T(8,128)}, f32[16,640]{1,0:T(8,128)}) custom-call(f32[1560,128]{1,0:T(8,128)} %get-tuple-element.12.acc_ref, bf16[2,128,256]{2,1,0:T(8,128)(2,1)} %get-tuple-element.13.aeb_ref, f32[10,24,128]{2,1,0:T(8,128)} %concatenate.26.x_ref, s32[1,64]{1,0:T(1,128)} %bitcast.66, ...), custom_call_target="tpu_custom_call" | custom-call | tf_op jit(solution)/shard_map/edges/pallas_call | solution.py:364
  42.4 1.0 %constant_dynamic-slice_fusion.1 = f32[2,1,2,16,664]{4,3,2,1,0:T(8,128)S(1)} fusion(f32[2,2,2,16,664]{4,3,2,1,0:T(8,128)} %bitcast.54, s32[]{:T(128)S(6)} %select_n.101), kind=kLoop, calls=%fused_computation.33 | loop fusion | bytes 339972 | tf_op jit(solution)/shard_map/jit(dynamic_index_in_dim)/dynamic_slice | solution.py:373
  43.4 3.7 %collective-permute-start.8 = (f32[64,664]{1,0:T(8,128)S(1)}, f32[64,664]{1,0:T(8,128)S(1)}, u32[]{:S(2)}, u32[]{:S(2)}) collective-permute-start(f32[64,664]{1,0:T(8,128)S(1)} %bitcast.58), channel_id=1, source_target_pairs={{0,2},{1,3},{2,0},{3,1},{4,6},{5,7},{6,4},{7,5},{8,10},{9,11},{10,... | collective-permute-start | bytes 509960 | tf_op jit(solution)/shard_map/ppermute | solution.py:341
  48.4 3.4 %collective-permute-done.11 = f32[16,640]{1,0:T(8,128)S(1)} collective-permute-done((f32[16,640]{1,0:T(8,128)S(1)}, f32[16,640]{1,0:T(8,128)S(1)}, u32[]{:S(2)}, u32[]{:S(2)}) %collective-permute-start.11) | collective-permute-done | bytes 40992 | tf_op jit(solution)/shard_map/ppermute | solution.py:341
  52.2 1.0 %constant_dynamic-slice_fusion.3 = f32[2,2,1,16,896]{4,3,2,1,0:T(8,128)S(1)} fusion(f32[2,2,2,16,896]{4,3,2,1,0:T(8,128)} %bitcast.52, s32[]{:T(128)S(6)} %select_n.97), kind=kLoop, calls=%fused_computation.35 | loop fusion | bytes 458756 | tf_op jit(solution)/shard_map/jit(dynamic_index_in_dim)/dynamic_slice | solution.py:373
  54.0 1.8 %collective-permute-done.12 = f32[16,640]{1,0:T(8,128)S(1)} collective-permute-done((f32[16,640]{1,0:T(8,128)S(1)}, f32[16,640]{1,0:T(8,128)S(1)}, u32[]{:S(2)}, u32[]{:S(2)}) %collective-permute-start.12) | collective-permute-done | bytes 40992 | tf_op jit(solution)/shard_map/ppermute | solution.py:341
  55.9 1.0 bitcast_add_fusion.1
  57.5 3.4 %collective-permute-done.6 = f32[64,896]{1,0:T(8,128)S(1)} collective-permute-done((f32[64,896]{1,0:T(8,128)S(1)}, f32[64,896]{1,0:T(8,128)S(1)}, u32[]{:S(2)}, u32[]{:S(2)}) %collective-permute-start.6) | collective-permute-done | bytes 229408 | tf_op jit(solution)/shard_map/ppermute | solution.py:341
  61.0 1.7 %collective-permute-start.7 = (f32[32,896]{1,0:T(8,128)S(1)}, f32[32,896]{1,0:T(8,128)S(1)}, u32[]{:S(2)}, u32[]{:S(2)}) collective-permute-start(f32[32,896]{1,0:T(8,128)S(1)} %bitcast.62), channel_id=1, source_target_pairs={{0,2},{1,3},{2,0},{3,1},{4,6},{5,7},{6,4},{7,5},{8,10},{9,11},{10,... | collective-permute-start | bytes 344072 | tf_op jit(solution)/shard_map/ppermute | solution.py:341
  62.7 3.1 %collective-permute-done.7 = f32[32,896]{1,0:T(8,128)S(1)} collective-permute-done((f32[32,896]{1,0:T(8,128)S(1)}, f32[32,896]{1,0:T(8,128)S(1)}, u32[]{:S(2)}, u32[]{:S(2)}) %collective-permute-start.7) | collective-permute-done | bytes 114720 | tf_op jit(solution)/shard_map/ppermute | solution.py:341
  66.0 3.9 %collective-permute-start.13 = (f32[16,2200]{1,0:T(8,128)S(1)}, f32[16,2200]{1,0:T(8,128)S(1)}, u32[]{:S(2)}, u32[]{:S(2)}) collective-permute-start(f32[16,2200]{1,0:T(8,128)S(1)} %pad_maximum_fusion.2), channel_id=1, source_target_pairs={{0,4},{1,5},{2,6},{3,7},{4,0},{5,1},{6,2},{7,3},{8,12},{9,13},{10,... | collective-permute-start | bytes 422408 | tf_op jit(solution)/shard_map/ppermute | solution.py:341
  70.4 4.2 %collective-permute-done.13 = f32[16,2200]{1,0:T(8,128)S(1)} collective-permute-done((f32[16,2200]{1,0:T(8,128)S(1)}, f32[16,2200]{1,0:T(8,128)S(1)}, u32[]{:S(2)}, u32[]{:S(2)}) %collective-permute-start.13) | collective-permute-done | bytes 140832 | tf_op jit(solution)/shard_map/ppermute | solution.py:341
  75.2 2.0 %fit.1 = f32[16,24]{1,0:T(8,128)} custom-call(f32[16,1560]{1,0:T(8,128)} %fusion.6.n_ref), custom_call_target="tpu_custom_call" | custom-call | tf_op jit(solution)/shard_map/fit/pallas_call | solution.py:402
  80.1 4.1 %model.1 = f32[64,512]{1,0:T(8,128)} custom-call(f32[16,640]{1,0:T(8,128)} %slice_add_fusion.nb_ref, f32[10,24,512]{2,1,0:T(8,128)} %pad_maximum_fusion.1.t_ref, f32[10,24,128]{2,1,0:T(8,128)} %concatenate.26.x_ref, f32[10,24,512]{2,1,0:T(8,128)} %copy-done.4, f32[10,24,128]{2,1,0:T(8,128)} %copy-done.8, f32[13,64,512]{2,1,0:T(8,128)} %copy-done, ...), custom_call_target="tpu_custom_call" | custom-call | tf_op jit(solution)/shard_map/model/pallas_call | solution.py:397
  84.2 4.1 %all-to-all-start = ((f32[8,8,512]{2,1,0:T(8,128)}), f32[8,8,512]{2,1,0:T(8,128)S(1)}, u32[]{:S(2)}, u32[]{:S(2)}) async-start(f32[8,8,512]{2,1,0:T(8,128)} %bitcast.48), calls=%async_computation | async-start | bytes 262144 | tf_op jit(solution)/shard_map/all_to_all | solution.py:401
  89.2 6.8 %all-to-all-done = f32[8,8,512]{2,1,0:T(8,128)S(1)} async-done(((f32[8,8,512]{2,1,0:T(8,128)}), f32[8,8,512]{2,1,0:T(8,128)S(1)}, u32[]{:S(2)}, u32[]{:S(2)}) %all-to-all-start) | async-done | bytes 131104 | tf_op jit(solution)/shard_map/all_to_all | solution.py:401
  (79 shorter events, 12.0 us)
Async XLA Ops:
  2.4 16.0 %copy-start = (f32[13,64,512]{2,1,0:T(8,128)}, f32[13,64,512]{2,1,0:T(8,128)S(1)}, u32[]{:S(2)}) copy-start(f32[13,64,512]{2,1,0:T(8,128)S(1)} %pad_maximum_fusion.own_ref.pack_ref) | copy-start | bytes 5111812
  2.4 16.0 %collective-permute-start.1 = (f32[13,64,512]{2,1,0:T(8,128)S(1)}, f32[13,64,512]{2,1,0:T(8,128)}, u32[]{:S(2)}, u32[]{:S(2)}) collective-permute-start(f32[13,64,512]{2,1,0:T(8,128)S(1)} %pad_maximum_fusion.own_ref.pack_ref), channel_id=1, source_target_pairs={{0,8},{8,0},{16,24},{24,16},{1,9},{9,1},{17,25},{25,17},{2,10},{10... | collective-permute-start | bytes 5111816 | tf_op jit(solution)/shard_map/ppermute | solution.py:341
  3.0 14.4 %collective-permute-start = (f32[120,512]{1,0:T(8,128)S(1)}, f32[120,512]{1,0:T(8,128)S(1)}, u32[]{:S(2)}, u32[]{:S(2)}) collective-permute-start(f32[120,512]{1,0:T(8,128)S(1)} %reshape.87), channel_id=1, source_target_pairs={{0,16},{8,24},{16,0},{24,8},{1,17},{9,25},{17,1},{25,9},{2,18},{10... | collective-permute-start | bytes 737288 | tf_op jit(solution)/shard_map/ppermute | solution.py:341
  6.1 6.3 %collective-permute-start.2 = (f32[10,120]{1,0:T(8,128)S(1)}, f32[10,120]{1,0:T(8,128)S(1)}, u32[]{:S(2)}, u32[]{:S(2)}) collective-permute-start(f32[10,120]{1,0:T(8,128)S(1)} %reshape.89), channel_id=1, source_target_pairs={{0,16},{8,24},{16,0},{24,8},{1,17},{9,25},{17,1},{25,9},{2,18},{10... | collective-permute-start | bytes 14408 | tf_op jit(solution)/shard_map/ppermute | solution.py:341
  6.2 32.7 %collective-permute-start.5 = (s32[1,64]{1,0:T(1,128)S(1)}, s32[1,64]{1,0:T(1,128)S(1)}, u32[]{:S(2)}, u32[]{:S(2)}) collective-permute-start(s32[1,64]{1,0:T(1,128)S(1)} %bitcast.68), channel_id=1, source_target_pairs={{0,8},{8,0},{16,24},{24,16},{1,9},{9,1},{17,25},{25,17},{2,10},{10... | collective-permute-start | bytes 776 | tf_op jit(solution)/shard_map/ppermute | solution.py:341
  12.5 24.8 %collective-permute-start.3 = (f32[5,240]{1,0:T(8,128)S(1)}, f32[5,240]{1,0:T(8,128)S(1)}, u32[]{:S(2)}, u32[]{:S(2)}) collective-permute-start(f32[5,240]{1,0:T(8,128)S(1)} %get-tuple-element.25), channel_id=1, source_target_pairs={{0,1},{1,2},{2,3},{3,4},{4,5},{5,6},{6,7},{8,9},{9,10},{10,11},{11... | collective-permute-start | bytes 14408 | tf_op jit(solution)/shard_map/ppermute | solution.py:350
  16.1 21.2 %collective-permute-start.4 = (f32[5,240]{1,0:T(8,128)S(1)}, f32[5,240]{1,0:T(8,128)S(1)}, u32[]{:S(2)}, u32[]{:S(2)}) collective-permute-start(f32[5,240]{1,0:T(8,128)S(1)} %get-tuple-element.24), channel_id=1, source_target_pairs={{1,0},{2,1},{3,2},{4,3},{5,4},{6,5},{7,6},{9,8},{10,9},{11,10},{12... | collective-permute-start | bytes 14408 | tf_op jit(solution)/shard_map/ppermute | solution.py:351
  42.4 18.5 %copy-start.5 = (f32[128,896]{1,0:T(8,128)S(1)}, f32[128,896]{1,0:T(8,128)}, u32[]{:S(2)}) copy-start(f32[128,896]{1,0:T(8,128)} %get-tuple-element.16) | copy-start | bytes 1376260
  42.4 4.7 %collective-permute-start.10 = (f32[16,640]{1,0:T(8,128)}, f32[16,640]{1,0:T(8,128)S(1)}, u32[]{:S(2)}, u32[]{:S(2)}) collective-permute-start(f32[16,640]{1,0:T(8,128)} %get-tuple-element.19), channel_id=1, source_target_pairs={{0,8},{8,0},{16,24},{24,16},{1,9},{9,1},{17,25},{25,17},{2,10},{10... | collective-permute-start | bytes 122888 | tf_op jit(solution)/shard_map/ppermute | solution.py:341
  43.4 12.5 %collective-permute-start.8 = (f32[64,664]{1,0:T(8,128)S(1)}, f32[64,664]{1,0:T(8,128)S(1)}, u32[]{:S(2)}, u32[]{:S(2)}) collective-permute-start(f32[64,664]{1,0:T(8,128)S(1)} %bitcast.58), channel_id=1, source_target_pairs={{0,2},{1,3},{2,0},{3,1},{4,6},{5,7},{6,4},{7,5},{8,10},{9,11},{10,... | collective-permute-start | bytes 509960 | tf_op jit(solution)/shard_map/ppermute | solution.py:341
  47.9 4.0 %collective-permute-start.11 = (f32[16,640]{1,0:T(8,128)S(1)}, f32[16,640]{1,0:T(8,128)S(1)}, u32[]{:S(2)}, u32[]{:S(2)}) collective-permute-start(f32[16,640]{1,0:T(8,128)S(1)} %add.95), channel_id=1, source_target_pairs={{0,1},{1,0},{2,3},{3,2},{4,5},{5,4},{6,7},{7,6},{8,9},{9,8},{10,11... | collective-permute-start | bytes 122888 | tf_op jit(solution)/shard_map/ppermute | solution.py:341
  51.9 4.0 %collective-permute-start.12 = (f32[16,640]{1,0:T(8,128)S(1)}, f32[16,640]{1,0:T(8,128)S(1)}, u32[]{:S(2)}, u32[]{:S(2)}) collective-permute-start(f32[16,640]{1,0:T(8,128)S(1)} %add.96), channel_id=1, source_target_pairs={{0,2},{1,3},{2,0},{3,1},{4,6},{5,7},{6,4},{7,5},{8,10},{9,11},{10,... | collective-permute-start | bytes 122888 | tf_op jit(solution)/shard_map/ppermute | solution.py:341
  52.2 17.6 %copy-start.1 = (f32[10,24,512]{2,1,0:T(8,128)S(1)}, f32[10,24,512]{2,1,0:T(8,128)}, u32[]{:S(2)}) copy-start(f32[10,24,512]{2,1,0:T(8,128)} %pad_maximum_fusion.1.t_ref) | copy-start | bytes 1474564
  52.2 17.6 %copy-start.3 = (f32[10,24,128]{2,1,0:T(8,128)S(1)}, f32[10,24,128]{2,1,0:T(8,128)}, u32[]{:S(2)}) copy-start(f32[10,24,128]{2,1,0:T(8,128)} %concatenate.26.x_ref) | copy-start | bytes 368644
  53.2 7.7 %collective-permute-start.6 = (f32[64,896]{1,0:T(8,128)S(1)}, f32[64,896]{1,0:T(8,128)S(1)}, u32[]{:S(2)}, u32[]{:S(2)}) collective-permute-start(f32[64,896]{1,0:T(8,128)S(1)} %bitcast.57), channel_id=1, source_target_pairs={{0,1},{1,0},{2,3},{3,2},{4,5},{5,4},{6,7},{7,6},{8,9},{9,8},{10,11... | collective-permute-start | bytes 688136 | tf_op jit(solution)/shard_map/ppermute | solution.py:341
  56.9 5.8 %collective-permute-start.9 = (f32[32,664]{1,0:T(8,128)S(1)}, f32[32,664]{1,0:T(8,128)S(1)}, u32[]{:S(2)}, u32[]{:S(2)}) collective-permute-start(f32[32,664]{1,0:T(8,128)S(1)} %bitcast.64), channel_id=1, source_target_pairs={{0,1},{1,0},{2,3},{3,2},{4,5},{5,4},{6,7},{7,6},{8,9},{9,8},{10,11... | collective-permute-start | bytes 254984 | tf_op jit(solution)/shard_map/ppermute | solution.py:341
  61.0 4.9 %collective-permute-start.7 = (f32[32,896]{1,0:T(8,128)S(1)}, f32[32,896]{1,0:T(8,128)S(1)}, u32[]{:S(2)}, u32[]{:S(2)}) collective-permute-start(f32[32,896]{1,0:T(8,128)S(1)} %bitcast.62), channel_id=1, source_target_pairs={{0,2},{1,3},{2,0},{3,1},{4,6},{5,7},{6,4},{7,5},{8,10},{9,11},{10,... | collective-permute-start | bytes 344072 | tf_op jit(solution)/shard_map/ppermute | solution.py:341
  66.0 8.6 %collective-permute-start.13 = (f32[16,2200]{1,0:T(8,128)S(1)}, f32[16,2200]{1,0:T(8,128)S(1)}, u32[]{:S(2)}, u32[]{:S(2)}) collective-permute-start(f32[16,2200]{1,0:T(8,128)S(1)} %pad_maximum_fusion.2), channel_id=1, source_target_pairs={{0,4},{1,5},{2,6},{3,7},{4,0},{5,1},{6,2},{7,3},{8,12},{9,13},{10,... | collective-permute-start | bytes 422408 | tf_op jit(solution)/shard_map/ppermute | solution.py:341
  69.8 8.8 %collective-permute-start.15 = (f32[10,24,512]{2,1,0:T(8,128)S(1)}, f32[10,24,512]{2,1,0:T(8,128)S(1)}, u32[]{:S(2)}, u32[]{:S(2)}) collective-permute-start(f32[10,24,512]{2,1,0:T(8,128)S(1)} %copy-done.1), channel_id=1, source_target_pairs={{0,8},{8,0},{16,24},{24,16},{1,9},{9,1},{17,25},{25,17},{2,10},{10... | collective-permute-start | bytes 1474568 | tf_op jit(solution)/shard_map/ppermute | solution.py:341
  69.8 8.8 %collective-permute-start.16 = (f32[10,24,128]{2,1,0:T(8,128)S(1)}, f32[10,24,128]{2,1,0:T(8,128)S(1)}, u32[]{:S(2)}, u32[]{:S(2)}) collective-permute-start(f32[10,24,128]{2,1,0:T(8,128)S(1)} %copy-done.3), channel_id=1, source_target_pairs={{0,8},{8,0},{16,24},{24,16},{1,9},{9,1},{17,25},{25,17},{2,10},{10... | collective-permute-start | bytes 368648 | tf_op jit(solution)/shard_map/ppermute | solution.py:341
  77.9 10.4 %collective-permute-start.14 = (f32[8,24]{1,0:T(8,128)S(1)}, f32[8,24]{1,0:T(8,128)S(1)}, u32[]{:S(2)}, u32[]{:S(2)}) collective-permute-start(f32[8,24]{1,0:T(8,128)S(1)} %get-tuple-element.27), channel_id=1, source_target_pairs={{0,8},{8,0},{16,24},{24,16},{1,9},{9,1},{17,25},{25,17},{2,10},{10... | collective-permute-start | bytes 2312 | tf_op jit(solution)/shard_map/ppermute | solution.py:341
  78.7 17.3 %copy-start.6 = (f32[8,3,4096]{2,0,1:T(8,128)S(1)}, f32[8,3,4096]{2,0,1:T(8,128)}, u32[]{:S(2)}) copy-start(f32[8,3,4096]{2,0,1:T(8,128)} %param.12) | copy-start | bytes 1179652
  78.7 17.3 %copy-start.7 = (s32[8,3,4096]{2,0,1:T(8,128)S(1)}, s32[8,3,4096]{2,0,1:T(8,128)}, u32[]{:S(2)}) copy-start(s32[8,3,4096]{2,0,1:T(8,128)} %param.13) | copy-start | bytes 1179652
  84.2 11.7 %all-to-all-start = ((f32[8,8,512]{2,1,0:T(8,128)}), f32[8,8,512]{2,1,0:T(8,128)S(1)}, u32[]{:S(2)}, u32[]{:S(2)}) async-start(f32[8,8,512]{2,1,0:T(8,128)} %bitcast.48), calls=%async_computation | async-start | bytes 262144 | tf_op jit(solution)/shard_map/all_to_all | solution.py:401
  (5 other events, 9.8 us)
